TPU v7x, 128 devices: a whole 4x4x4 slice. The times are simulated.
128 devices in a mesh: batch: 4 (over y), seq: 32 (over z, x, core).
Axes of the slice: x: 4, y: 4, z: 4, core: 2. Of those that a mesh axis runs over, the one named last changes fastest.
Arguments:
- queries: bfloat16 [4, 8192, 1024], P('batch', 'seq'), may hold values from -6 to 6
- key_states: bfloat16 [4, 8192, 1024], P('batch', 'seq'), may hold values from -6 to 6
- value_states: bfloat16 [4, 8192, 1024], P('batch', 'seq'), may hold values from -6 to 6
- out_grad: bfloat16 [4, 8192, 1024], P('batch', 'seq'), may hold values from -6 to 6
- memory: float32 [1024, 1024], replicated, may hold values from -6 to 6
- near_device: int32 [64, 8], replicated, may hold values from 0 to 31, all different within a row; in each aligned block of 2 rows (0 to 1, 2 to 3, ...) no two rows name the same one
- near_slot: int32 [64, 8], replicated, may hold values from 0 to 1
- near_count: int32 [64], replicated, may hold values from 1 to 8, 288 in all
- writer_block: int32 [1024], replicated, may hold values from 0 to 63, as said below
Outputs:
- attended: bfloat16 [4, 8192, 1024], P('batch', 'seq')
- query_grad: bfloat16 [4, 8192, 1024], P('batch', 'seq')
- key_grad: bfloat16 [4, 8192, 1024], P('batch', 'seq')
- value_grad: bfloat16 [4, 8192, 1024], P('batch', 'seq')
- memory_grad: float32 [1024, 1024], P('seq')
Inputs may be any that keep to these rules, and one draw needn't show every extreme that they name: Row n of near_device belongs to block n; one row names different indices; the rows of the 2 blocks of one index of seq name no index more than 1 times. writer_block[r] // 2 == r // 32: a memory row is written by a block of the index of seq that holds the row.
All inputs are finite; a program needn't handle non-finite values.
Results may differ from a plain program's by a relative error of at most 0.025.
Values may be sent and summed in bfloat16 or wider, within the bound.
No kernel may reach another device: no remote copies, remote signals or barrier semaphores. Data moves between devices by JAX's collectives and lax.ppermute only.
A program may use at most 192 MiB of HBM per device.

v0:
```python
import math

import jax
import jax.numpy as jnp
from jax import lax
from jax.sharding import PartitionSpec as P

HEADS = 8
HD = 128
BLK = 128
MEM = 1024


def route_tables(near_device, near_slot, seq_devices):
    target = near_device.reshape(seq_devices, -1)
    source_slot = near_slot.reshape(seq_devices, -1)
    position = jnp.arange(target.shape[1])
    earlier = position[None, :] < position[:, None]
    matching = target[:, :, None] == target[:, None, :]
    arrival = jnp.sum(jnp.logical_and(matching, earlier[None, :, :]), axis=2)
    return (target, source_slot, arrival)


def shards(
    queries,
    key_states,
    value_states,
    out_grad,
    memory,
    near_device,
    near_slot,
    near_count,
    writer_block,
):
    seq_devices = lax.axis_size("seq")
    my_index = lax.axis_index("seq")
    tokens = queries.shape[1]
    row_width = queries.shape[2]
    near_width = near_device.shape[1]
    local_blocks = tokens // BLK
    entries = local_blocks * near_width
    capacity = (entries + seq_devices - 1) // seq_devices
    rows_dev = MEM // seq_devices
    key_scaling_factor = 1.0 / math.sqrt(HD)
    block_scale = 1.0 / math.sqrt(BLK)
    value_blocks = value_states[0].reshape(local_blocks, BLK, row_width)
    key_blocks = key_states[0].reshape(local_blocks, BLK, row_width)
    value_sums = jnp.sum(value_blocks, axis=1, dtype=jnp.float32)
    my_writers = (
        lax.dynamic_slice_in_dim(writer_block, my_index * rows_dev, rows_dev, 0)
        - my_index * local_blocks
    )
    mine = lax.dynamic_slice_in_dim(memory, my_index * rows_dev, rows_dev, 0)
    written = (mine + jnp.take(value_sums, my_writers, axis=0) * block_scale).astype(jnp.bfloat16)
    memory_keys = lax.all_gather(written, "seq", axis=0, tiled=True)
    target, source_slot, arrival = route_tables(near_device, near_slot, seq_devices)
    my_target = lax.dynamic_index_in_dim(target, my_index, 0, keepdims=False)
    my_arrival = lax.dynamic_index_in_dim(arrival, my_index, 0, keepdims=False)
    flat_place = my_target * capacity + my_arrival
    entry_slot = (flat_place[:, None] == jnp.arange(seq_devices * capacity)[None, :]).astype(
        jnp.bfloat16
    )
    toward_me = (target == my_index).astype(jnp.float32)
    arrival_hot = (arrival[:, :, None] == jnp.arange(capacity)[None, None, :]).astype(jnp.float32)
    slot_hot = (source_slot[:, :, None] == jnp.arange(local_blocks)[None, None, :]).astype(
        jnp.float32
    )
    select = jnp.einsum("de,des,del->dsl", toward_me, arrival_hot, slot_hot).astype(jnp.bfloat16)
    send_keys = jnp.einsum(
        "dsl,ltw->dstw", select, key_blocks, preferred_element_type=jnp.float32
    ).astype(jnp.bfloat16)
    send_values = jnp.einsum(
        "dsl,ltw->dstw", select, value_blocks, preferred_element_type=jnp.float32
    ).astype(jnp.bfloat16)
    got_keys, got_values = (
        lax.all_to_all(send_keys, "seq", split_axis=0, concat_axis=0, tiled=True),
        lax.all_to_all(send_values, "seq", split_axis=0, concat_axis=0, tiled=True),
    )
    flat_keys = got_keys.reshape(seq_devices * capacity, BLK, row_width)
    flat_values = got_values.reshape(seq_devices * capacity, BLK, row_width)
    neighbour_key_rows = jnp.einsum(
        "ef,ftw->etw", entry_slot, flat_keys, preferred_element_type=jnp.float32
    ).astype(jnp.bfloat16)
    neighbour_value_rows = jnp.einsum(
        "ef,ftw->etw", entry_slot, flat_values, preferred_element_type=jnp.float32
    ).astype(jnp.bfloat16)
    neighbour_key_rows = neighbour_key_rows.reshape(local_blocks, near_width * BLK, HEADS, HD)
    neighbour_value_rows = neighbour_value_rows.reshape(local_blocks, near_width * BLK, HEADS, HD)
    my_count = lax.dynamic_slice_in_dim(near_count, my_index * local_blocks, local_blocks, 0)
    live_keys = jnp.arange(near_width * BLK)[None, :] // BLK < my_count[:, None]
    query_head_states = queries[0].reshape(local_blocks, BLK, HEADS, HD)
    head_output_gradient = out_grad[0].reshape(local_blocks, BLK, HEADS, HD)
    memory_head_states = memory_keys.reshape(MEM, HEADS, HD)
    memory_score_logits = (
        jnp.einsum(
            "xswr,gwr->xwsg",
            query_head_states,
            memory_head_states,
            preferred_element_type=jnp.float32,
        )
        * key_scaling_factor
    )
    score_near = (
        jnp.einsum(
            "cqhd,ckhd->chqk",
            query_head_states,
            neighbour_key_rows,
            preferred_element_type=jnp.float32,
        )
        * key_scaling_factor
    )
    score_near = jnp.where(live_keys[:, None, None, :], score_near, -jnp.inf)
    row_max = jnp.maximum(jnp.max(memory_score_logits, axis=-1), jnp.max(score_near, axis=-1))
    exp_mem = jnp.exp(memory_score_logits - row_max[..., None])
    exp_near = jnp.exp(score_near - row_max[..., None])
    row_total = jnp.sum(exp_mem, axis=-1) + jnp.sum(exp_near, axis=-1)
    prob_mem = exp_mem / row_total[..., None]
    prob_near = exp_near / row_total[..., None]
    memory_attention_weight = prob_mem.astype(jnp.bfloat16)
    neighbour_attention_weight = prob_near.astype(jnp.bfloat16)
    head_attended_output = (
        jnp.einsum(
            "vjpe,eji->vpji",
            memory_attention_weight,
            memory_head_states,
            preferred_element_type=jnp.float32,
        )
        + jnp.einsum(
            "chqk,ckhd->cqhd",
            neighbour_attention_weight,
            neighbour_value_rows,
            preferred_element_type=jnp.float32,
        )
    ).astype(jnp.bfloat16)
    grad_dot = jnp.einsum(
        "cqhd,cqhd->chq",
        head_output_gradient,
        head_attended_output,
        preferred_element_type=jnp.float32,
    )
    memory_probability_gradient = jnp.einsum(
        "xswr,gwr->xwsg",
        head_output_gradient,
        memory_head_states,
        preferred_element_type=jnp.float32,
    )
    dprob_near = jnp.einsum(
        "cqhd,ckhd->chqk",
        head_output_gradient,
        neighbour_value_rows,
        preferred_element_type=jnp.float32,
    )
    memory_score_gradient = (prob_mem * (memory_probability_gradient - grad_dot[..., None])).astype(
        jnp.bfloat16
    )
    neighbour_score_gradient = (prob_near * (dprob_near - grad_dot[..., None])).astype(jnp.bfloat16)
    query_portion = (
        jnp.einsum(
            "vjpe,eji->vpji",
            memory_score_gradient,
            memory_head_states,
            preferred_element_type=jnp.float32,
        )
        + jnp.einsum(
            "chqk,ckhd->cqhd",
            neighbour_score_gradient,
            neighbour_key_rows,
            preferred_element_type=jnp.float32,
        )
    ) * key_scaling_factor
    key_part = (
        jnp.einsum(
            "chqk,cqhd->ckhd",
            neighbour_score_gradient,
            query_head_states,
            preferred_element_type=jnp.float32,
        )
        * key_scaling_factor
    ).astype(jnp.bfloat16)
    value_part = jnp.einsum(
        "chqk,cqhd->ckhd",
        neighbour_attention_weight,
        head_output_gradient,
        preferred_element_type=jnp.float32,
    ).astype(jnp.bfloat16)
    key_part = key_part.reshape(entries, BLK, row_width)
    value_part = value_part.reshape(entries, BLK, row_width)
    back_keys = jnp.einsum(
        "ef,etw->ftw", entry_slot, key_part, preferred_element_type=jnp.float32
    ).astype(jnp.bfloat16)
    back_values = jnp.einsum(
        "ef,etw->ftw", entry_slot, value_part, preferred_element_type=jnp.float32
    ).astype(jnp.bfloat16)
    back_keys = back_keys.reshape(seq_devices, capacity, BLK, row_width)
    back_values = back_values.reshape(seq_devices, capacity, BLK, row_width)
    slot_keys_grad, slot_values_grad = (
        lax.all_to_all(back_keys, "seq", split_axis=0, concat_axis=0, tiled=True),
        lax.all_to_all(back_values, "seq", split_axis=0, concat_axis=0, tiled=True),
    )
    key_sum = jnp.einsum(
        "dsl,dstw->ltw", select, slot_keys_grad, preferred_element_type=jnp.float32
    )
    value_sum = jnp.einsum(
        "dsl,dstw->ltw", select, slot_values_grad, preferred_element_type=jnp.float32
    )
    term = (
        jnp.einsum(
            "irey,ierk->yrk",
            memory_score_gradient,
            query_head_states,
            preferred_element_type=jnp.float32,
        )
        * key_scaling_factor
    )
    term = term + jnp.einsum(
        "irey,ierk->yrk",
        memory_attention_weight,
        head_output_gradient,
        preferred_element_type=jnp.float32,
    )
    row_grads = lax.psum_scatter(
        term.reshape(lax.axis_size("seq") * rows_dev, row_width).astype(jnp.bfloat16),
        "seq",
        scatter_dimension=0,
        tiled=True,
    ).astype(jnp.float32)
    writer_match = (my_writers[:, None] == jnp.arange(local_blocks)[None, :])[:, :, None]
    spread = jnp.sum(jnp.where(writer_match, row_grads[:, None, :], 0.0), axis=0) * block_scale
    memory_grad = lax.psum(row_grads.astype(jnp.bfloat16), "batch").astype(jnp.float32)
    attended = head_attended_output.reshape(1, tokens, row_width)
    query_grad = query_portion.astype(jnp.bfloat16).reshape(1, tokens, row_width)
    key_grad = key_sum.astype(jnp.bfloat16).reshape(1, tokens, row_width)
    value_grad = (value_sum + spread[:, None, :]).astype(jnp.bfloat16).reshape(1, tokens, row_width)
    return (attended, query_grad, key_grad, value_grad, memory_grad)


def solution(mesh):
    placed = (
        P("batch", "seq", None),
        P("batch", "seq", None),
        P("batch", "seq", None),
        P("batch", "seq", None),
        P(),
        P(),
        P(),
        P(),
        P(),
    )
    return jax.shard_map(
        shards,
        mesh=mesh,
        in_specs=placed,
        out_specs=(
            P("batch", "seq", None),
            P("batch", "seq", None),
            P("batch", "seq", None),
            P("batch", "seq", None),
            P("seq", None),
        ),
        check_vma=False,
    )
```

profile of v0, /device:TPU:7, one launch (start us, length us, event | category | flops | bytes accessed | tf_op | source)
XLA Modules:
  0.0 692.0 jit_solution(7028056440561422739)
XLA Ops:
  9.6 6.7 convert_bitcast_fusion.2
  16.2 11.3 %copy.205 = bf16[32,1,128,1024]{3,2,1,0:T(8,128)(2,1)} copy(bf16[32,1,128,1024]{3,0,2,1:T(8,128)(2,1)} %convert_bitcast_fusion.2) | data formatting | bytes 16777216 | tf_op jit(solution)/shard_map/convert_element_type | solution.py:74
  27.5 9.1 %all-to-all-start.1 = ((bf16[32,1,128,1024]{3,2,1,0:T(8,128)(2,1)}), bf16[32,1,128,1024]{3,2,1,0:T(8,128)(2,1)}, u32[]{:S(2)}, u32[]{:S(2)}) async-start(bf16[32,1,128,1024]{3,2,1,0:T(8,128)(2,1)} %copy.205), calls=%async_computation.1 | async-start | bytes 16777216 | tf_op jit(solution)/shard_map/all_to_all | solution.py:77
  36.7 4.7 convert_bitcast_fusion.3
  41.4 11.3 %copy.197 = bf16[32,1,128,1024]{3,2,1,0:T(8,128)(2,1)} copy(bf16[32,1,128,1024]{3,0,2,1:T(8,128)(2,1)} %convert_bitcast_fusion.3) | data formatting | bytes 16777216 | tf_op jit(solution)/shard_map/convert_element_type | solution.py:71
  52.7 85.1 %all-to-all-done.1 = bf16[32,1,128,1024]{3,2,1,0:T(8,128)(2,1)} async-done(((bf16[32,1,128,1024]{3,2,1,0:T(8,128)(2,1)}), bf16[32,1,128,1024]{3,2,1,0:T(8,128)(2,1)}, u32[]{:S(2)}, u32[]{:S(2)}) %all-to-all-start.1) | async-done | bytes 8388640 | tf_op jit(solution)/shard_map/all_to_all | solution.py:77
  137.7 9.5 %all-to-all-start = ((bf16[32,1,128,1024]{3,2,1,0:T(8,128)(2,1)}), bf16[32,1,128,1024]{3,2,1,0:T(8,128)(2,1)}, u32[]{:S(2)}, u32[]{:S(2)}) async-start(bf16[32,1,128,1024]{3,2,1,0:T(8,128)(2,1)} %copy.197), calls=%async_computation | async-start | bytes 16777216 | tf_op jit(solution)/shard_map/all_to_all | solution.py:76
  148.7 1.6 add_convert_fusion
  152.5 98.4 %all-gather.2.cloned.1.call-done = bf16[1024,1024]{1,0:T(8,128)(2,1)} async-done(((bf16[32,1024]{1,0:T(8,128)(2,1)}), bf16[1024,1024]{1,0:T(8,128)(2,1)}) %all-gather.2.cloned.1.call-update) | async-done | bytes 2097168 | tf_op jit(solution)/shard_map/all_gather | solution.py:55
  250.9 3.1 copy.187
  254.0 4.5 bitcast_reduce_fusion.1
  258.5 12.4 %fusion.38 = bf16[16,128,1024]{2,0,1:T(8,128)(2,1)S(1)} fusion(bf16[32,1,128,1024]{3,2,1,0:T(8,128)(2,1)} %all-to-all-done.1, s32[16]{0:T(128)S(1)} %add_reduce_fusion), kind=kOutput, calls=%fused_computation.48 | convolution fusion | flops 136315392 | bytes 12582976 | tf_op jit(solution)/shard_map/ef,ftw->etw/dot_general | solution.py:84
  270.9 2.7 copy.207
  273.6 3.1 copy.283
  276.7 12.4 %fusion.35 = bf16[16,128,1024]{2,0,1:T(8,128)(2,1)S(1)} fusion(bf16[32,1,128,1024]{3,2,1,0:T(8,128)(2,1)} %all-to-all-done, s32[16]{0:T(128)S(1)} %add_reduce_fusion), kind=kOutput, calls=%fused_computation.47 | convolution fusion | flops 136315392 | bytes 12582976 | tf_op jit(solution)/shard_map/ef,ftw->etw/dot_general | solution.py:81
  289.1 2.5 copy.199
  291.6 3.1 copy.282
  294.7 6.7 copy.217
  301.3 4.1 bitcast_reduce_fusion
  305.5 8.4 %fusion.20 = (f32[2,8,128]{2,0,1:T(2,128)S(1)}, f32[2,8,128]{2,0,1:T(2,128)S(1)}) fusion(f32[2,8,1024,128]{3,2,0,1:T(8,128)S(1)} %get-tuple-element.12, f32[2,8,128]{2,0,1:T(2,128)S(1)} %max.7, pred[2,1024]{1,0:T(4,128)(4,1)S(1)} %broadcast_compare_fusion, f32[8,1024,2,128]{3,1,2,0:T(8,128)} %get-tuple-element.10), kind=kLoop, calls=%fused_computation.33 | loop fusion | flops 14675968 | bytes 16803840 | tf_op jit(solution)/shard_map/reduce_sum | solution.py:116
  314.0 2.2 fusion.44
  317.8 2.3 slice-done.1
  320.1 3.1 bitcast_convert_fusion
  323.1 2.5 copy.257
  325.7 1.6 multiply_reduce_fusion
  327.3 6.9 fusion.4
  334.2 1.9 copy-done.5
  337.4 4.7 copy.223
  342.1 7.7 %reshape.214 = bf16[16,128,1024]{2,1,0:T(8,128)(2,1)} reshape(bf16[2,1024,8,128]{3,2,1,0:T(8,128)(2,1)} %copy.223) | data formatting | bytes 8388608 | tf_op jit(solution)/shard_map/reshape | solution.py:186
  349.8 8.8 %convert_bitcast_fusion.1 = bf16[32,1,128,1024]{3,0,2,1:T(8,128)(2,1)} fusion(bf16[16,128,1024]{2,1,0:T(8,128)(2,1)} %reshape.214, s32[16]{0:T(128)S(1)} %add_reduce_fusion), kind=kOutput, calls=%fused_computation.25 | convolution fusion | flops 138412544 | bytes 12582976 | tf_op jit(solution)/shard_map/ef,etw->ftw/dot_general | solution.py:188
  358.6 11.3 %copy.225 = bf16[32,1,128,1024]{3,2,1,0:T(8,128)(2,1)} copy(bf16[32,1,128,1024]{3,0,2,1:T(8,128)(2,1)} %convert_bitcast_fusion.1) | data formatting | bytes 16777216 | tf_op jit(solution)/shard_map/reshape | solution.py:194
  369.9 6.9 all-to-all-start.2
  376.7 3.4 convert_bitcast_fusion.4
  380.2 4.7 copy.230
  384.9 7.3 %reshape.218 = bf16[16,128,1024]{2,1,0:T(8,128)(2,1)} reshape(bf16[2,1024,8,128]{3,2,1,0:T(8,128)(2,1)} %copy.230) | data formatting | bytes 8388608 | tf_op jit(solution)/shard_map/reshape | solution.py:187
  392.1 8.8 %convert_bitcast_fusion = bf16[32,1,128,1024]{3,0,2,1:T(8,128)(2,1)} fusion(bf16[16,128,1024]{2,1,0:T(8,128)(2,1)} %reshape.218, s32[16]{0:T(128)S(1)} %add_reduce_fusion), kind=kOutput, calls=%fused_computation.24 | convolution fusion | flops 138412544 | bytes 12582976 | tf_op jit(solution)/shard_map/ef,etw->ftw/dot_general | solution.py:191
  400.9 11.3 %copy.232 = bf16[32,1,128,1024]{3,2,1,0:T(8,128)(2,1)} copy(bf16[32,1,128,1024]{3,0,2,1:T(8,128)(2,1)} %convert_bitcast_fusion) | data formatting | bytes 16777216 | tf_op jit(solution)/shard_map/reshape | solution.py:195
  412.2 65.6 %all-to-all-done.2 = bf16[32,1,128,1024]{3,2,1,0:T(8,128)(2,1)} async-done(((bf16[32,1,128,1024]{3,2,1,0:T(8,128)(2,1)}), bf16[32,1,128,1024]{3,2,1,0:T(8,128)(2,1)}, u32[]{:S(2)}, u32[]{:S(2)}) %all-to-all-start.2) | async-done | bytes 8388640 | tf_op jit(solution)/shard_map/all_to_all | solution.py:197
  477.8 9.5 %all-to-all-start.3 = ((bf16[32,1,128,1024]{3,2,1,0:T(8,128)(2,1)}), bf16[32,1,128,1024]{3,2,1,0:T(8,128)(2,1)}, u32[]{:S(2)}, u32[]{:S(2)}) async-start(bf16[32,1,128,1024]{3,2,1,0:T(8,128)(2,1)} %copy.232), calls=%async_computation.3 | async-start | bytes 16777216 | tf_op jit(solution)/shard_map/all_to_all | solution.py:198
  487.4 5.2 fusion.6
  492.6 2.0 copy-done.7
  496.1 7.0 %fusion.22 = bf16[8,1024,128]{1,2,0:T(8,128)(2,1)} fusion(f32[8,1024,128,1]{1,2,3,0:T(8,128)S(1)} %fusion.90, bf16[2,128,8,128]{1,3,0,2:T(8,128)(2,1)S(1)} %copy-done.12, f32[8,1024,2,128]{3,1,2,0:T(8,128)} %get-tuple-element.10, f32[2,8,128]{2,0,1:T(2,128)S(1)} %add.76, f32[2,8,128]{2,0,1:T(2,128)S(1)} %max.7), kind=kOutput, calls=%fused_computation.36 | convolution fusion | flops 548405248 | bytes 15220736 | tf_op jit(solution)/shard_map/irey,ierk->yrk/dot_general | solution.py:215
  503.1 3.9 copy.238
  509.5 3.2 convolution_bitcast_fusion.1
  516.8 94.8 %reduce-scatter.2.cloned.1.call-done = bf16[32,1024]{1,0:T(8,128)(2,1)} async-done(((bf16[1024,1024]{1,0:T(8,128)(2,1)}), bf16[32,1024]{1,0:T(8,128)(2,1)}) %reduce-scatter.2.cloned.1.call-update) | async-done | bytes 65552 | tf_op jit(solution)/shard_map/reduce_scatter | solution.py:221
  613.3 43.3 %all-reduce.2.cloned.1.call-done = bf16[32,1024]{1,0:T(8,128)(2,1)} async-done(((bf16[32,1024]{1,0:T(8,128)(2,1)}), bf16[32,1024]{1,0:T(8,128)(2,1)}) %all-reduce.2.cloned.1.call-update) | async-done | bytes 65552 | tf_op jit(solution)/shard_map/psum | solution.py:229
  658.2 12.5 %fusion.57 = bf16[2,128,1024]{2,0,1:T(2,128)(2,1)S(1)} fusion(bf16[32,1,128,1024]{3,2,1,0:T(8,128)(2,1)} %all-to-all-done.2, bf16[32,2]{0,1:T(2,128)(2,1)S(1)} %copy-done.14), kind=kOutput, calls=%fused_computation.61 | convolution fusion | flops 17039360 | bytes 8913024 | tf_op jit(solution)/shard_map/dsl,dstw->ltw/dot_general | solution.py:200
  671.6 12.8 %fusion.66 = bf16[2,128,1024]{2,0,1:T(2,128)(2,1)S(1)} fusion(bf16[32,1,128,1024]{3,2,1,0:T(8,128)(2,1)} %all-to-all-done.3, f32[2,1024]{1,0:T(2,128)S(1)} %broadcast_multiply_fusion, bf16[32,2]{0,1:T(2,128)(2,1)S(1)} %copy-done.14), kind=kOutput, calls=%fused_computation.64 | convolution fusion | flops 17301504 | bytes 8921216 | tf_op jit(solution)/shard_map/dsl,dstw->ltw/dot_general | solution.py:203
  (84 shorter events, 22.1 us)
Async XLA Ops:
  7.2 29.5 %copy-start = (bf16[1,256,1024]{2,1,0:T(8,128)(2,1)S(1)}, bf16[1,256,1024]{2,1,0:T(8,128)(2,1)}, u32[]{:S(2)}) copy-start(bf16[1,256,1024]{2,1,0:T(8,128)(2,1)} %param.10) | copy-start | bytes 1572868
  9.6 27.1 %copy-start.13 = (bf16[32,2]{0,1:T(2,128)(2,1)}, bf16[32,2]{0,1:T(2,128)(2,1)S(1)}, u32[]{:S(2)}) copy-start(bf16[32,2]{0,1:T(2,128)(2,1)S(1)} %copy.285) | copy-start | bytes 388
  27.5 110.2 %all-to-all-start.1 = ((bf16[32,1,128,1024]{3,2,1,0:T(8,128)(2,1)}), bf16[32,1,128,1024]{3,2,1,0:T(8,128)(2,1)}, u32[]{:S(2)}, u32[]{:S(2)}) async-start(bf16[32,1,128,1024]{3,2,1,0:T(8,128)(2,1)} %copy.205), calls=%async_computation.1 | async-start | bytes 16777216 | tf_op jit(solution)/shard_map/all_to_all | solution.py:77
  52.7 95.4 %copy-start.9 = (bf16[1,256,1024]{2,1,0:T(8,128)(2,1)S(1)}, bf16[1,256,1024]{2,1,0:T(8,128)(2,1)}, u32[]{:S(2)}) copy-start(bf16[1,256,1024]{2,1,0:T(8,128)(2,1)} %param.11) | copy-start | bytes 1572868
  52.7 97.7 %copy-start.10 = (bf16[1,256,1024]{2,1,0:T(8,128)(2,1)S(1)}, bf16[1,256,1024]{2,1,0:T(8,128)(2,1)}, u32[]{:S(2)}) copy-start(bf16[1,256,1024]{2,1,0:T(8,128)(2,1)} %param.12) | copy-start | bytes 1572868
  52.7 99.0 %copy-start.11 = (bf16[1,256,1024]{2,1,0:T(8,128)(2,1)S(1)}, bf16[1,256,1024]{2,1,0:T(8,128)(2,1)}, u32[]{:S(2)}) copy-start(bf16[1,256,1024]{2,1,0:T(8,128)(2,1)} %param.9) | copy-start | bytes 1572868
  52.7 99.5 %copy-start.15 = (s32[64]{0:T(128)S(1)}, s32[64]{0:T(128)}, u32[]{:S(2)}) copy-start(s32[64]{0:T(128)} %param.16) | copy-start | bytes 772
  137.7 139.0 %all-to-all-start = ((bf16[32,1,128,1024]{3,2,1,0:T(8,128)(2,1)}), bf16[32,1,128,1024]{3,2,1,0:T(8,128)(2,1)}, u32[]{:S(2)}, u32[]{:S(2)}) async-start(bf16[32,1,128,1024]{3,2,1,0:T(8,128)(2,1)} %copy.197), calls=%async_computation | async-start | bytes 16777216 | tf_op jit(solution)/shard_map/all_to_all | solution.py:76
  147.2 103.7 %all-gather.2.cloned.1.call-start = ((), (), s32[]{:S(2)}) async-start(), calls=%async_computation.5 | async-start | bytes 2162688 | tf_op jit(solution)/shard_map/all_gather | solution.py:55
  305.4 8.5 %copy-start.2 = (f32[2,8,1024,128]{3,2,0,1:T(8,128)}, f32[2,8,1024,128]{3,2,0,1:T(8,128)S(1)}, u32[]{:S(2)}) copy-start(f32[2,8,1024,128]{3,2,0,1:T(8,128)S(1)} %get-tuple-element.12) | copy-start | bytes 25165828
  313.9 2.3 copy-start.8
  313.9 3.9 slice-start
  313.9 6.1 slice-start.1
  316.2 7.0 %copy-start.4 = (bf16[2,8,128,1024]{2,3,0,1:T(8,128)(2,1)}, bf16[2,8,128,1024]{2,3,0,1:T(8,128)(2,1)S(1)}, u32[]{:S(2)}) copy-start(bf16[2,8,128,1024]{2,3,0,1:T(8,128)(2,1)S(1)} %fusion.44) | copy-start | bytes 12582916
  334.2 1.9 copy-start.5
  369.9 108.0 %all-to-all-start.2 = ((bf16[32,1,128,1024]{3,2,1,0:T(8,128)(2,1)}), bf16[32,1,128,1024]{3,2,1,0:T(8,128)(2,1)}, u32[]{:S(2)}, u32[]{:S(2)}) async-start(bf16[32,1,128,1024]{3,2,1,0:T(8,128)(2,1)} %copy.225), calls=%async_computation.2 | async-start | bytes 16777216 | tf_op jit(solution)/shard_map/all_to_all | solution.py:197
  412.2 75.1 %copy-start.12 = (bf16[2,128,8,128]{1,3,0,2:T(8,128)(2,1)S(1)}, bf16[2,128,8,128]{1,3,0,2:T(8,128)(2,1)}, u32[]{:S(2)}) copy-start(bf16[2,128,8,128]{1,3,0,2:T(8,128)(2,1)} %copy.237) | copy-start | bytes 1572868
  477.8 193.8 %all-to-all-start.3 = ((bf16[32,1,128,1024]{3,2,1,0:T(8,128)(2,1)}), bf16[32,1,128,1024]{3,2,1,0:T(8,128)(2,1)}, u32[]{:S(2)}, u32[]{:S(2)}) async-start(bf16[32,1,128,1024]{3,2,1,0:T(8,128)(2,1)} %copy.232), calls=%async_computation.3 | async-start | bytes 16777216 | tf_op jit(solution)/shard_map/all_to_all | solution.py:198
  487.3 124.3 %reduce-scatter.2.cloned.1.call-start = ((), (), s32[]{:S(2)}) async-start(), calls=%async_computation.6 | async-start | bytes 2162688 | tf_op jit(solution)/shard_map/reduce_scatter | solution.py:221
  492.6 2.0 copy-start.7
  509.5 3.4 copy-start.3
  509.5 4.7 copy-start.6
  514.2 144.0 %copy-start.14 = (bf16[32,2]{0,1:T(2,128)(2,1)S(1)}, bf16[32,2]{0,1:T(2,128)(2,1)}, u32[]{:S(2)}) copy-start(bf16[32,2]{0,1:T(2,128)(2,1)} %copy-done.13) | copy-start | bytes 388
  612.4 44.2 %all-reduce.2.cloned.1.call-start = ((), (), s32[]{:S(2)}) async-start(), calls=%async_computation.7 | async-start | bytes 131072 | tf_op jit(solution)/shard_map/psum | solution.py:229
  656.6 28.7 %copy-start.1 = (bf16[1,256,1024]{2,1,0:T(8,128)(2,1)S(1)}, bf16[1,256,1024]{2,1,0:T(8,128)(2,1)}, u32[]{:S(2)}) copy-start(bf16[1,256,1024]{2,1,0:T(8,128)(2,1)} %param.10) | copy-start | bytes 1572868
Sparse Core Ops, SparseCore 0:
  150.8 99.9 all-gather.1
  507.2 104.3 reduce-scatter.1
  615.6 41.0 all-reduce.1
where the time goes:
time: 702 us; the launch traced here: 692 us
  waiting for transfers between devices  388 us (55%)
  matrix products  122 us (17%)
  local copies, waits for them, and re-layouts  115 us (16%)
  starting transfers between devices  35.4 us (5%)
  other arithmetic  17.9 us (3%)
  between operations  14.3 us (2%)
    all_gather x1, waiting for transfers between devices, shards(): memory_keys = lax.all_gather(written, 'seq', axis=0, tiled=True)  98.4 us
    reduce_scatter x1, waiting for transfers between devices, shards(): lax.psum_scatter(term.reshape(lax.axis_size('seq') * rows_dev, row_width)...  94.8 us
    all_to_all x1, waiting for transfers between devices, shards(): lax.all_to_all(send_values, 'seq', split_axis=0, concat_axis=0, tiled=True)  85.1 us
    all_to_all x1, waiting for transfers between devices, shards(): lax.all_to_all(back_keys, 'seq', split_axis=0, concat_axis=0, tiled=True)  65.6 us
    psum x1, waiting for transfers between devices, shards(): lax.psum(row_grads.astype(jnp.bfloat16), 'batch').astype(jnp.float32)  43.3 us
    unnamed x45, local copies, waits for them, and re-layouts  18.6 us
  transfers between devices with their start and end apart: 7, of which 5 were waited for; matrix products, arithmetic and copies ran while one was open for 18% of the time, Pallas kernels for 0%

commit v1 on v0

--- a/solution.py
+++ b/solution.py
@@ -9,16 +9,6 @@
 HD = 128
 BLK = 128
 MEM = 1024
-
-
-def route_tables(near_device, near_slot, seq_devices):
-    target = near_device.reshape(seq_devices, -1)
-    source_slot = near_slot.reshape(seq_devices, -1)
-    position = jnp.arange(target.shape[1])
-    earlier = position[None, :] < position[:, None]
-    matching = target[:, :, None] == target[:, None, :]
-    arrival = jnp.sum(jnp.logical_and(matching, earlier[None, :, :]), axis=2)
-    return (target, source_slot, arrival)
 
 
 def shards(
@@ -33,59 +23,43 @@
     writer_block,
 ):
     seq_devices = lax.axis_size("seq")
+    batch_devices = lax.axis_size("batch")
     my_index = lax.axis_index("seq")
     tokens = queries.shape[1]
     row_width = queries.shape[2]
     near_width = near_device.shape[1]
     local_blocks = tokens // BLK
     entries = local_blocks * near_width
-    capacity = (entries + seq_devices - 1) // seq_devices
     rows_dev = MEM // seq_devices
     key_scaling_factor = 1.0 / math.sqrt(HD)
     block_scale = 1.0 / math.sqrt(BLK)
     value_blocks = value_states[0].reshape(local_blocks, BLK, row_width)
     key_blocks = key_states[0].reshape(local_blocks, BLK, row_width)
+
+    target = near_device.reshape(seq_devices, entries)
+    source_slot = near_slot.reshape(seq_devices, entries)
+    my_target = lax.dynamic_index_in_dim(target, my_index, 0, keepdims=False)
+    names_me = target == my_index
+    send_idx = jnp.sum(jnp.where(names_me, source_slot, 0), axis=1)
+    kv_blocks = jnp.stack([key_blocks, value_blocks], axis=1)
+    send_kv = jnp.take(kv_blocks, send_idx, axis=0)
+    got_kv = lax.all_to_all(send_kv, "seq", split_axis=0, concat_axis=0, tiled=True)
+
     value_sums = jnp.sum(value_blocks, axis=1, dtype=jnp.float32)
-    my_writers = (
-        lax.dynamic_slice_in_dim(writer_block, my_index * rows_dev, rows_dev, 0)
-        - my_index * local_blocks
-    )
-    mine = lax.dynamic_slice_in_dim(memory, my_index * rows_dev, rows_dev, 0)
-    written = (mine + jnp.take(value_sums, my_writers, axis=0) * block_scale).astype(jnp.bfloat16)
-    memory_keys = lax.all_gather(written, "seq", axis=0, tiled=True)
-    target, source_slot, arrival = route_tables(near_device, near_slot, seq_devices)
-    my_target = lax.dynamic_index_in_dim(target, my_index, 0, keepdims=False)
-    my_arrival = lax.dynamic_index_in_dim(arrival, my_index, 0, keepdims=False)
-    flat_place = my_target * capacity + my_arrival
-    entry_slot = (flat_place[:, None] == jnp.arange(seq_devices * capacity)[None, :]).astype(
+    all_sums = lax.all_to_all(
+        jnp.broadcast_to(value_sums[None], (seq_devices, local_blocks, row_width)),
+        "seq",
+        split_axis=0,
+        concat_axis=0,
+        tiled=True,
+    ).reshape(seq_devices * local_blocks, row_width)
+    memory_keys = (memory + jnp.take(all_sums, writer_block, axis=0) * block_scale).astype(
         jnp.bfloat16
     )
-    toward_me = (target == my_index).astype(jnp.float32)
-    arrival_hot = (arrival[:, :, None] == jnp.arange(capacity)[None, None, :]).astype(jnp.float32)
-    slot_hot = (source_slot[:, :, None] == jnp.arange(local_blocks)[None, None, :]).astype(
-        jnp.float32
-    )
-    select = jnp.einsum("de,des,del->dsl", toward_me, arrival_hot, slot_hot).astype(jnp.bfloat16)
-    send_keys = jnp.einsum(
-        "dsl,ltw->dstw", select, key_blocks, preferred_element_type=jnp.float32
-    ).astype(jnp.bfloat16)
-    send_values = jnp.einsum(
-        "dsl,ltw->dstw", select, value_blocks, preferred_element_type=jnp.float32
-    ).astype(jnp.bfloat16)
-    got_keys, got_values = (
-        lax.all_to_all(send_keys, "seq", split_axis=0, concat_axis=0, tiled=True),
-        lax.all_to_all(send_values, "seq", split_axis=0, concat_axis=0, tiled=True),
-    )
-    flat_keys = got_keys.reshape(seq_devices * capacity, BLK, row_width)
-    flat_values = got_values.reshape(seq_devices * capacity, BLK, row_width)
-    neighbour_key_rows = jnp.einsum(
-        "ef,ftw->etw", entry_slot, flat_keys, preferred_element_type=jnp.float32
-    ).astype(jnp.bfloat16)
-    neighbour_value_rows = jnp.einsum(
-        "ef,ftw->etw", entry_slot, flat_values, preferred_element_type=jnp.float32
-    ).astype(jnp.bfloat16)
-    neighbour_key_rows = neighbour_key_rows.reshape(local_blocks, near_width * BLK, HEADS, HD)
-    neighbour_value_rows = neighbour_value_rows.reshape(local_blocks, near_width * BLK, HEADS, HD)
+
+    neighbour_kv = jnp.take(got_kv, my_target, axis=0)
+    neighbour_key_rows = neighbour_kv[:, 0].reshape(local_blocks, near_width * BLK, HEADS, HD)
+    neighbour_value_rows = neighbour_kv[:, 1].reshape(local_blocks, near_width * BLK, HEADS, HD)
     my_count = lax.dynamic_slice_in_dim(near_count, my_index * local_blocks, local_blocks, 0)
     live_keys = jnp.arange(near_width * BLK)[None, :] // BLK < my_count[:, None]
     query_head_states = queries[0].reshape(local_blocks, BLK, HEADS, HD)
@@ -185,24 +159,6 @@
     ).astype(jnp.bfloat16)
     key_part = key_part.reshape(entries, BLK, row_width)
     value_part = value_part.reshape(entries, BLK, row_width)
-    back_keys = jnp.einsum(
-        "ef,etw->ftw", entry_slot, key_part, preferred_element_type=jnp.float32
-    ).astype(jnp.bfloat16)
-    back_values = jnp.einsum(
-        "ef,etw->ftw", entry_slot, value_part, preferred_element_type=jnp.float32
-    ).astype(jnp.bfloat16)
-    back_keys = back_keys.reshape(seq_devices, capacity, BLK, row_width)
-    back_values = back_values.reshape(seq_devices, capacity, BLK, row_width)
-    slot_keys_grad, slot_values_grad = (
-        lax.all_to_all(back_keys, "seq", split_axis=0, concat_axis=0, tiled=True),
-        lax.all_to_all(back_values, "seq", split_axis=0, concat_axis=0, tiled=True),
-    )
-    key_sum = jnp.einsum(
-        "dsl,dstw->ltw", select, slot_keys_grad, preferred_element_type=jnp.float32
-    )
-    value_sum = jnp.einsum(
-        "dsl,dstw->ltw", select, slot_values_grad, preferred_element_type=jnp.float32
-    )
     term = (
         jnp.einsum(
             "irey,ierk->yrk",
@@ -218,15 +174,44 @@
         head_output_gradient,
         preferred_element_type=jnp.float32,
     )
-    row_grads = lax.psum_scatter(
-        term.reshape(lax.axis_size("seq") * rows_dev, row_width).astype(jnp.bfloat16),
-        "seq",
-        scatter_dimension=0,
-        tiled=True,
-    ).astype(jnp.float32)
+    term = term.reshape(seq_devices, rows_dev, row_width).astype(jnp.bfloat16)
+
+    hits = my_target[None, :] == jnp.arange(seq_devices)[:, None]
+    inverse = jnp.sum(jnp.where(hits, jnp.arange(entries)[None, :], 0), axis=1)
+    valid = jnp.any(hits, axis=1)[:, None, None]
+    back_keys = jnp.where(valid, jnp.take(key_part, inverse, axis=0), jnp.zeros((), jnp.bfloat16))
+    back_values = jnp.where(valid, jnp.take(value_part, inverse, axis=0), jnp.zeros((), jnp.bfloat16))
+    back = jnp.concatenate([back_keys, back_values, term], axis=1)
+    got_back = lax.all_to_all(back, "seq", split_axis=0, concat_axis=0, tiled=True)
+    select = jnp.sum(
+        jnp.where(
+            names_me[:, :, None],
+            (source_slot[:, :, None] == jnp.arange(local_blocks)[None, None, :]).astype(jnp.float32),
+            0.0,
+        ),
+        axis=1,
+    ).astype(jnp.bfloat16)
+    key_sum = jnp.einsum(
+        "dl,dtw->ltw", select, got_back[:, :BLK], preferred_element_type=jnp.float32
+    )
+    value_sum = jnp.einsum(
+        "dl,dtw->ltw", select, got_back[:, BLK : 2 * BLK], preferred_element_type=jnp.float32
+    )
+    row_grads = jnp.sum(got_back[:, 2 * BLK :].astype(jnp.float32), axis=0)
+    my_writers = (
+        lax.dynamic_slice_in_dim(writer_block, my_index * rows_dev, rows_dev, 0)
+        - my_index * local_blocks
+    )
     writer_match = (my_writers[:, None] == jnp.arange(local_blocks)[None, :])[:, :, None]
     spread = jnp.sum(jnp.where(writer_match, row_grads[:, None, :], 0.0), axis=0) * block_scale
-    memory_grad = lax.psum(row_grads.astype(jnp.bfloat16), "batch").astype(jnp.float32)
+    all_rows = lax.all_to_all(
+        jnp.broadcast_to(row_grads[None], (batch_devices, rows_dev, row_width)),
+        "batch",
+        split_axis=0,
+        concat_axis=0,
+        tiled=True,
+    )
+    memory_grad = jnp.sum(all_rows, axis=0)
     attended = head_attended_output.reshape(1, tokens, row_width)
     query_grad = query_portion.astype(jnp.bfloat16).reshape(1, tokens, row_width)
     key_grad = key_sum.astype(jnp.bfloat16).reshape(1, tokens, row_width)

time: 702 us -> 708 us (level)
  matrix products: 122 us -> 63.1 us
  other arithmetic: 17.9 us -> 71.9 us
  waiting for transfers between devices: 388 us -> 412 us
  between operations: 14.3 us -> 1.59 us
    all_to_all x4, waiting for transfers between devices: 151 us -> 412 us  [the longest x1 225 us: shards(): lax.all_to_all(back, 'seq', split_axis=0, concat_axis=0, tiled=True)]
    all_gather x1 -> x0, waiting for transfers between devices: 98.4 us -> none  [shards(): memory_keys = lax.all_gather(written, 'seq', axis=0, tiled=True)]
    reduce_scatter x1 -> x0, waiting for transfers between devices: 94.8 us -> none  [shards(): lax.psum_scatter(term.reshape(lax.axis_size('seq') * rows_dev, row_width)...]
    dot_general x8 -> x2, matrix products: 78.9 us -> 21.7 us  [the longest x1 12.6 us: shards(): jnp.einsum('dl,dtw->ltw', select, got_back[:, BLK:2 * BLK], preferred_ele...]
    psum x1 -> x0, waiting for transfers between devices: 43.3 us -> none  [shards(): lax.psum(row_grads.astype(jnp.bfloat16), 'batch').astype(jnp.float32)]
    gather x1 -> x5, local copies, waits for them, and re-layouts: 0.61 us -> 37.4 us  [the longest x1 10.5 us: shards(): neighbour_kv = jnp.take(got_kv, my_target, axis=0)]
    select_n x1 -> x6, other arithmetic: 0.01 us -> 33.6 us  [the longest x2 14.2 us: shards(): send_kv = jnp.take(kv_blocks, send_idx, axis=0)]
    convert_element_type x5 -> x2, local copies, waits for them, and re-layouts: 31.8 us -> 5.49 us  [shards(): term = term.reshape(seq_devices, rows_dev, row_width).astype(jnp.bfloat16)]
  transfers between devices with their start and end apart: 7 -> 4, of which waited for: 5 -> 2; matrix products, arithmetic and copies ran while one was open for 18% -> 9% of each run, Pallas kernels for 0% -> 0%
where the time goes in v1:
time: 708 us; the launch traced here: 698 us
  waiting for transfers between devices  412 us (58%)
  local copies, waits for them, and re-layouts  115 us (16%)
  other arithmetic  71.9 us (10%)
  matrix products  63.1 us (9%)
  starting transfers between devices  34.5 us (5%)
    all_to_all x1, waiting for transfers between devices, shards(): lax.all_to_all(back, 'seq', split_axis=0, concat_axis=0, tiled=True)  225 us
    all_to_all x1, waiting for transfers between devices, shards(): lax.all_to_all(send_kv, 'seq', split_axis=0, concat_axis=0, tiled=True)  186 us
    unnamed x56, local copies, waits for them, and re-layouts  14.5 us
    concatenate x1, other arithmetic, shards(): back = jnp.concatenate([back_keys, back_values, term], axis=1)  14.3 us
    select_n x2, other arithmetic, shards(): send_kv = jnp.take(kv_blocks, send_idx, axis=0)  14.2 us
  transfers between devices with their start and end apart: 4, of which 2 were waited for; matrix products, arithmetic and copies ran while one was open for 9% of the time, Pallas kernels for 0%

profile of v1, /device:TPU:7, one launch (start us, length us, event | category | flops | bytes accessed | tf_op | source)
XLA Modules:
  0.0 698.0 jit_solution(738143510924904912)
XLA Ops:
  2.5 8.7 %all-to-all-start = ((f32[32,2,1024]{2,1,0:T(2,128)}), f32[32,2,1024]{2,1,0:T(2,128)S(1)}, u32[]{:S(2)}, u32[]{:S(2)}) async-start(f32[32,2,1024]{2,1,0:T(2,128)} %broadcast_in_dim.150), calls=%async_computation | async-start | bytes 524288 | tf_op jit(solution)/shard_map/all_to_all | solution.py:49
  12.2 1.3 pad_maximum_fusion.1
  13.5 7.1 %gather_fusion.1 = bf16[32,2,128,1024]{3,2,1,0:T(8,128)(2,1)} fusion(bf16[2,2,128,1024]{3,2,0,1:T(8,128)(2,1)S(1)} %pad_maximum_fusion.1, s32[1024]{0:T(1024)S(1)} %pad_clamp_fusion.2), kind=kCustom, calls=%fused_computation.3 | custom fusion | bytes 33554560 | tf_op jit(solution)/shard_map/jit(_take)/gather | solution.py:45
  20.6 14.2 %broadcast_select_fusion = bf16[32,2,128,1024]{3,2,1,0:T(8,128)(2,1)} fusion(bf16[32,2,128,1024]{3,2,1,0:T(8,128)(2,1)} %gather_fusion.1, pred[32]{0:T(512)(128)(4,1)S(1)} %compare_and_fusion.2), kind=kLoop, calls=%fused_computation.6 | loop fusion | flops 8388608 | bytes 33554464 | tf_op jit(solution)/shard_map/jit(_take)/select_n | solution.py:45
  34.9 7.9 %all-to-all-start.1 = ((bf16[32,2,128,1024]{3,2,1,0:T(8,128)(2,1)}), bf16[32,2,128,1024]{3,2,1,0:T(8,128)(2,1)}, u32[]{:S(2)}, u32[]{:S(2)}) async-start(bf16[32,2,128,1024]{3,2,1,0:T(8,128)(2,1)} %broadcast_select_fusion), calls=%async_computation.1 | async-start | bytes 33554432 | tf_op jit(solution)/shard_map/all_to_all | solution.py:46
  43.9 5.4 gather_fusion
  49.3 4.2 fusion.25
  54.1 3.0 copy.193
  57.1 4.5 bitcast_reduce_fusion.1
  61.6 186.5 %all-to-all-done.1 = bf16[32,2,128,1024]{3,2,1,0:T(8,128)(2,1)} async-done(((bf16[32,2,128,1024]{3,2,1,0:T(8,128)(2,1)}), bf16[32,2,128,1024]{3,2,1,0:T(8,128)(2,1)}, u32[]{:S(2)}, u32[]{:S(2)}) %all-to-all-start.1) | async-done | bytes 16777248 | tf_op jit(solution)/shard_map/all_to_all | solution.py:46
  248.0 10.5 %gather_fusion.2 = bf16[16,2,128,1024]{3,2,1,0:T(8,128)(2,1)} fusion(bf16[32,2,128,1024]{3,2,1,0:T(8,128)(2,1)} %all-to-all-done.1, s32[1024]{0:T(1024)S(1)} %pad_clamp_fusion.1), kind=kCustom, calls=%fused_computation.4 | custom fusion | bytes 16777280 | tf_op jit(solution)/shard_map/jit(_take)/gather | solution.py:60
  258.6 7.5 %broadcast_select_fusion.1 = bf16[16,2,128,1024]{3,2,1,0:T(8,128)(2,1)} fusion(bf16[16,2,128,1024]{3,2,1,0:T(8,128)(2,1)} %gather_fusion.2, pred[16]{0:T(512)(128)(4,1)S(1)} %get-tuple-element.8), kind=kLoop, calls=%fused_computation.26 | loop fusion | flops 4194304 | bytes 16777232 | tf_op jit(solution)/shard_map/jit(_take)/select_n | solution.py:60
  266.0 5.2 fusion.86
  271.3 3.0 copy.232
  274.3 6.7 copy.169
  281.0 4.1 bitcast_reduce_fusion
  285.1 8.4 %fusion.12 = (f32[2,8,128]{2,0,1:T(2,128)S(1)}, f32[2,8,128]{2,0,1:T(2,128)S(1)}) fusion(f32[2,8,1024,128]{3,2,0,1:T(8,128)S(1)} %get-tuple-element.19, f32[2,8,128]{2,0,1:T(2,128)S(1)} %max.7, pred[2,1024]{1,0:T(4,128)(4,1)S(1)} %broadcast_compare_fusion.1, f32[8,1024,2,128]{3,1,2,0:T(8,128)} %get-tuple-element.17), kind=kLoop, calls=%fused_computation.30 | loop fusion | flops 14675968 | bytes 16803840 | tf_op jit(solution)/shard_map/reduce_sum | solution.py:90
  293.6 2.7 fusion.35
  297.5 1.6 fusion.42
  299.1 2.3 slice-done
  303.3 3.1 bitcast_convert_fusion
  306.3 2.6 copy.202
  308.9 1.6 multiply_reduce_fusion
  310.6 5.1 fusion.6
  315.7 8.4 %fusion.4 = bf16[2,8,128,1024]{2,3,0,1:T(8,128)(2,1)} fusion(f32[2,8,128]{2,0,1:T(2,128)S(1)} %copy.203, bf16[2,1024,8,128]{3,2,1,0:T(8,128)(2,1)S(1)} %bitcast.163, f32[2,8,128]{2,0,1:T(2,128)S(1)} %add.105, f32[2,8,128]{2,0,1:T(2,128)S(1)} %max.7, f32[2,8,1024,128]{3,2,0,1:T(8,128)} %copy-done, pred[2,1024]{1,0:T(4,128)(4,1)S(1)} %broadcast_compare_fusion.1, ...), kind=kOutput, calls=%fused_computation.12 | convolution fusion | flops 551550976 | bytes 17328128 | tf_op jit(solution)/shard_map/cqhd,ckhd->chqk/dot_general | solution.py:121
  324.1 3.2 convert_bitcast_fusion
  329.5 2.4 fusion.32
  331.9 2.7 copy.184
  334.6 2.8 convert_element_type.84
  337.4 3.4 fusion.13
  340.8 4.7 copy.178
  345.5 7.3 %reshape.215 = bf16[16,128,1024]{2,1,0:T(8,128)(2,1)} reshape(bf16[2,1024,8,128]{3,2,1,0:T(8,128)(2,1)} %copy.178) | data formatting | bytes 8388608 | tf_op jit(solution)/shard_map/reshape | solution.py:160
  352.8 6.8 copy.181
  359.7 7.3 %reshape.216 = bf16[16,128,1024]{2,1,0:T(8,128)(2,1)} reshape(bf16[2,1024,8,128]{3,2,1,0:T(8,128)(2,1)} %copy.181) | data formatting | bytes 8388608 | tf_op jit(solution)/shard_map/reshape | solution.py:161
  367.0 7.2 %gather_fusion.3 = bf16[32,128,1024]{2,1,0:T(8,128)(2,1)} fusion(bf16[16,128,1024]{2,1,0:T(8,128)(2,1)} %reshape.215, s32[1024]{0:T(1024)S(1)} %pad_clamp_fusion), kind=kCustom, calls=%fused_computation.clone | custom fusion | bytes 16777344 | tf_op jit(solution)/shard_map/jit(_take)/gather | solution.py:182
  374.2 7.1 %gather_fusion.4 = bf16[32,128,1024]{2,1,0:T(8,128)(2,1)} fusion(bf16[16,128,1024]{2,1,0:T(8,128)(2,1)} %reshape.216, s32[1024]{0:T(1024)S(1)} %pad_clamp_fusion), kind=kCustom, calls=%fused_computation.1.clone | custom fusion | bytes 16777344 | tf_op jit(solution)/shard_map/jit(_take)/gather | solution.py:183
  381.3 11.9 %select_select_fusion.1 = (bf16[32,128,1024]{2,1,0:T(8,128)(2,1)}, bf16[32,128,1024]{2,1,0:T(8,128)(2,1)}) fusion(bf16[32,128,1024]{2,1,0:T(8,128)(2,1)} %gather_fusion.3, pred[32]{0:T(512)(128)(4,1)S(1)} %compare_and_fusion.1, pred[32]{0:T(512)(128)(4,1)S(1)} %fusion.70, bf16[32,128,1024]{2,1,0:T(8,128)(2,1)} %gather_fusion.4), kind=kLoop, calls=%fused_computation.23 | loop fusion | flops 16777216 | bytes 33554496 | tf_op jit(solution)/shard_map/jit(_where)/select_n | solution.py:182
  393.2 14.3 %pad_maximum_fusion = bf16[32,288,1024]{2,1,0:T(8,128)(2,1)} fusion(bf16[32,32,1024]{2,1,0:T(8,128)(2,1)S(1)} %convert_element_type.84, bf16[32,128,1024]{2,1,0:T(8,128)(2,1)} %get-tuple-element.15, bf16[32,128,1024]{2,1,0:T(8,128)(2,1)} %get-tuple-element.14), kind=kLoop, calls=%fused_computation.5 | loop fusion | flops 56623104 | bytes 37748736 | tf_op jit(solution)/shard_map/concatenate | solution.py:184
  407.5 13.4 %all-to-all-start.2 = ((bf16[32,288,1024]{2,1,0:T(8,128)(2,1)}), bf16[32,288,1024]{2,1,0:T(8,128)(2,1)}, u32[]{:S(2)}, u32[]{:S(2)}) async-start(bf16[32,288,1024]{2,1,0:T(8,128)(2,1)} %pad_maximum_fusion), calls=%async_computation.2 | async-start | bytes 37748736 | tf_op jit(solution)/shard_map/all_to_all | solution.py:185
  423.4 3.2 convolution_bitcast_fusion.1
  426.8 1.3 copy-done.2
  428.1 1.2 fusion.47
  430.7 225.5 %all-to-all-done.2 = bf16[32,288,1024]{2,1,0:T(8,128)(2,1)} async-done(((bf16[32,288,1024]{2,1,0:T(8,128)(2,1)}), bf16[32,288,1024]{2,1,0:T(8,128)(2,1)}, u32[]{:S(2)}, u32[]{:S(2)}) %all-to-all-start.2) | async-done | bytes 18874400 | tf_op jit(solution)/shard_map/all_to_all | solution.py:185
  656.1 9.7 %fusion.85 = (bf16[32,128,1024]{2,1,0:T(8,128)(2,1)}, bf16[32,128,1024]{2,1,0:T(8,128)(2,1)S(1)}) fusion(bf16[32,288,1024]{2,1,0:T(8,128)(2,1)} %all-to-all-done.2), kind=kLoop, calls=%fused_computation.120 | loop fusion | bytes 33554432 | tf_op jit(solution)/shard_map/slice | solution.py:198
  665.8 9.1 %fusion.48 = bf16[2,128,1024]{2,0,1:T(2,128)(2,1)S(1)} fusion(bf16[32,128,1024]{2,1,0:T(8,128)(2,1)S(1)} %get-tuple-element.11, bf16[32,2]{0,1:T(2,128)(2,1)S(1)} %select_reduce_fusion.1), kind=kOutput, calls=%fused_computation.61 | convolution fusion | flops 17039360 | bytes 8913024 | tf_op jit(solution)/shard_map/dl,dtw->ltw/dot_general | solution.py:194
  675.9 2.0 convert_reduce_fusion
  678.9 4.4 all-to-all-start.3
  683.3 12.6 %fusion.57 = bf16[2,128,1024]{2,0,1:T(2,128)(2,1)S(1)} fusion(bf16[32,128,1024]{2,1,0:T(8,128)(2,1)} %get-tuple-element.10, f32[2,1024]{1,0:T(2,128)S(1)} %broadcast_multiply_fusion, bf16[32,2]{0,1:T(2,128)(2,1)S(1)} %select_reduce_fusion.1), kind=kOutput, calls=%fused_computation.64 | convolution fusion | flops 17301504 | bytes 8921216 | tf_op jit(solution)/shard_map/dl,dtw->ltw/dot_general | solution.py:197
  (100 shorter events, 17.3 us)
Async XLA Ops:
  2.5 32.3 %all-to-all-start = ((f32[32,2,1024]{2,1,0:T(2,128)}), f32[32,2,1024]{2,1,0:T(2,128)S(1)}, u32[]{:S(2)}, u32[]{:S(2)}) async-start(f32[32,2,1024]{2,1,0:T(2,128)} %broadcast_in_dim.150), calls=%async_computation | async-start | bytes 524288 | tf_op jit(solution)/shard_map/all_to_all | solution.py:49
  34.8 8.0 %copy-start.17 = (s32[64,8]{0,1:T(8,128)S(1)}, s32[64,8]{0,1:T(8,128)}, u32[]{:S(2)}) copy-start(s32[64,8]{0,1:T(8,128)} %param.16) | copy-start | bytes 6148
  34.8 8.2 %copy-start.11 = (bf16[1,256,1024]{2,1,0:T(8,128)(2,1)S(1)}, bf16[1,256,1024]{2,1,0:T(8,128)(2,1)}, u32[]{:S(2)}) copy-start(bf16[1,256,1024]{2,1,0:T(8,128)(2,1)} %param.11) | copy-start | bytes 1572868
  34.8 8.3 %copy-start.12 = (bf16[1,256,1024]{2,1,0:T(8,128)(2,1)S(1)}, bf16[1,256,1024]{2,1,0:T(8,128)(2,1)}, u32[]{:S(2)}) copy-start(bf16[1,256,1024]{2,1,0:T(8,128)(2,1)} %param.14) | copy-start | bytes 1572868
  34.8 8.4 %copy-start.19 = (s32[64]{0:T(128)S(1)}, s32[64]{0:T(128)}, u32[]{:S(2)}) copy-start(s32[64]{0:T(128)} %param.18) | copy-start | bytes 772
  34.8 8.7 %copy-start.16 = (s32[1024]{0:T(1024)S(1)}, s32[1024]{0:T(1024)}, u32[]{:S(2)}) copy-start(s32[1024]{0:T(1024)} %param.19) | copy-start | bytes 12292
  34.9 213.2 %all-to-all-start.1 = ((bf16[32,2,128,1024]{3,2,1,0:T(8,128)(2,1)}), bf16[32,2,128,1024]{3,2,1,0:T(8,128)(2,1)}, u32[]{:S(2)}, u32[]{:S(2)}) async-start(bf16[32,2,128,1024]{3,2,1,0:T(8,128)(2,1)} %broadcast_select_fusion), calls=%async_computation.1 | async-start | bytes 33554432 | tf_op jit(solution)/shard_map/all_to_all | solution.py:46
  43.0 0.6 copy-start.14
  285.1 8.5 %copy-start = (f32[2,8,1024,128]{3,2,0,1:T(8,128)}, f32[2,8,1024,128]{3,2,0,1:T(8,128)S(1)}, u32[]{:S(2)}) copy-start(f32[2,8,1024,128]{3,2,0,1:T(8,128)S(1)} %get-tuple-element.19) | copy-start | bytes 25165828
  293.6 2.7 copy-start.8
  296.3 2.8 copy-start.3
  296.3 5.1 slice-start
  296.3 5.8 copy-start.9
  297.5 8.9 %copy-start.6 = (bf16[256,8,8,128]{3,2,1,0:T(8,128)(2,1)}, bf16[256,8,8,128]{3,2,1,0:T(8,128)(2,1)S(1)}, u32[]{:S(2)}) copy-start(bf16[256,8,8,128]{3,2,1,0:T(8,128)(2,1)S(1)} %copy.233) | copy-start | bytes 12582916
  297.5 5.8 slice-start.1
  310.5 5.1 copy-start.7
  315.6 11.6 %copy-start.5 = (bf16[2,8,128,1024]{2,3,0,1:T(8,128)(2,1)}, bf16[2,8,128,1024]{2,3,0,1:T(8,128)(2,1)S(1)}, u32[]{:S(2)}) copy-start(bf16[2,8,128,1024]{2,3,0,1:T(8,128)(2,1)S(1)} %fusion.6) | copy-start | bytes 12582916
  315.6 8.4 %copy-start.4 = (bf16[2,8,128,1024]{2,3,0,1:T(8,128)(2,1)S(1)}, bf16[2,8,128,1024]{2,3,0,1:T(8,128)(2,1)}, u32[]{:S(2)}) copy-start(bf16[2,8,128,1024]{2,3,0,1:T(8,128)(2,1)} %copy-done.3) | copy-start | bytes 12582916
  324.1 4.4 slice-start.2
  327.3 2.2 slice-start.3
  407.5 13.4 %copy-start.18 = (s32[64,8]{0,1:T(8,128)S(1)}, s32[64,8]{0,1:T(8,128)}, u32[]{:S(2)}) copy-start(s32[64,8]{0,1:T(8,128)} %param.17) | copy-start | bytes 6148
  407.5 13.7 %copy-start.15 = (s32[32,16]{1,0:T(8,128)S(1)}, s32[32,16]{1,0:T(8,128)}, u32[]{:S(2)}) copy-start(s32[32,16]{1,0:T(8,128)} %copy-done.14) | copy-start | bytes 6148
  407.5 14.6 %copy-start.13 = (bf16[2,128,8,128]{1,3,0,2:T(8,128)(2,1)S(1)}, bf16[2,128,8,128]{1,3,0,2:T(8,128)(2,1)}, u32[]{:S(2)}) copy-start(bf16[2,128,8,128]{1,3,0,2:T(8,128)(2,1)} %get-tuple-element.21) | copy-start | bytes 1572868
  407.5 15.9 %copy-start.10 = (bf16[1024,8,128,1]{0,2,3,1:T(8,128)(2,1)S(1)}, bf16[1024,8,128,1]{0,2,3,1:T(8,128)(2,1)}, u32[]{:S(2)}) copy-start(bf16[1024,8,128,1]{0,2,3,1:T(8,128)(2,1)} %copy.193) | copy-start | bytes 6291460
  407.5 248.6 %all-to-all-start.2 = ((bf16[32,288,1024]{2,1,0:T(8,128)(2,1)}), bf16[32,288,1024]{2,1,0:T(8,128)(2,1)}, u32[]{:S(2)}, u32[]{:S(2)}) async-start(bf16[32,288,1024]{2,1,0:T(8,128)(2,1)} %pad_maximum_fusion), calls=%async_computation.2 | async-start | bytes 37748736 | tf_op jit(solution)/shard_map/all_to_all | solution.py:185
  423.4 3.4 copy-start.1
  423.4 4.7 copy-start.2
  678.9 18.0 %all-to-all-start.3 = ((f32[4,32,1024]{2,1,0:T(8,128)}), f32[4,32,1024]{2,1,0:T(8,128)S(1)}, u32[]{:S(2)}, u32[]{:S(2)}) async-start(f32[4,32,1024]{2,1,0:T(8,128)} %broadcast_in_dim.169), calls=%async_computation.3 | async-start | bytes 1048576 | tf_op jit(solution)/shard_map/all_to_all | solution.py:207

commit v2 on v1

v2 whole, which is shorter than its diff:
```python
import math

import jax
import jax.numpy as jnp
from jax import lax
from jax.experimental import pallas as pl
from jax.experimental.pallas import tpu as pltpu
from jax.sharding import PartitionSpec as P

HEADS = 8
HD = 128
BLK = 128
MEM = 1024
NEAR = 8


def _attn_body(cnt_ref, tgt_ref, q_ref, do_ref, mk_ref, *rest):
    k_refs = rest[:NEAR]
    v_refs = rest[NEAR : 2 * NEAR]
    o_ref, dq_ref, dk_ref, dv_ref, tm_ref = rest[2 * NEAR :]
    n = pl.program_id(1)
    scale = 1.0 / math.sqrt(HD)
    f32 = jnp.float32
    nt = (((1,), (1,)), ((), ()))
    tn = (((0,), (0,)), ((), ()))
    q = q_ref[...]
    do = do_ref[...]
    mk = mk_ref[...]
    nk = jnp.concatenate([r[0, 0] for r in k_refs], axis=0)
    nv = jnp.concatenate([r[0, 0] for r in v_refs], axis=0)
    sm = lax.dot_general(q, mk, nt, preferred_element_type=f32) * scale
    sn = lax.dot_general(q, nk, nt, preferred_element_type=f32) * scale
    col = lax.broadcasted_iota(jnp.int32, sn.shape, 1) // BLK
    sn = jnp.where(col < cnt_ref[n], sn, -jnp.inf)
    m = jnp.maximum(jnp.max(sm, axis=1, keepdims=True), jnp.max(sn, axis=1, keepdims=True))
    em = jnp.exp(sm - m)
    en = jnp.exp(sn - m)
    total = jnp.sum(em, axis=1, keepdims=True) + jnp.sum(en, axis=1, keepdims=True)
    pm = em / total
    pn = en / total
    wm = pm.astype(jnp.bfloat16)
    wn = pn.astype(jnp.bfloat16)
    o = (
        jnp.dot(wm, mk, preferred_element_type=f32) + jnp.dot(wn, nv, preferred_element_type=f32)
    ).astype(jnp.bfloat16)
    o_ref[...] = o
    gd = jnp.sum(do.astype(f32) * o.astype(f32), axis=1, keepdims=True)
    dpm = lax.dot_general(do, mk, nt, preferred_element_type=f32)
    dpn = lax.dot_general(do, nv, nt, preferred_element_type=f32)
    dsm = (pm * (dpm - gd)).astype(jnp.bfloat16)
    dsn = (pn * (dpn - gd)).astype(jnp.bfloat16)
    dq_ref[...] = (
        (jnp.dot(dsm, mk, preferred_element_type=f32) + jnp.dot(dsn, nk, preferred_element_type=f32))
        * scale
    ).astype(jnp.bfloat16)
    dk_ref[0] = (lax.dot_general(dsn, q, tn, preferred_element_type=f32) * scale).astype(jnp.bfloat16)
    dv_ref[0] = lax.dot_general(wn, do, tn, preferred_element_type=f32).astype(jnp.bfloat16)
    tm = lax.dot_general(dsm, q, tn, preferred_element_type=f32) * scale + lax.dot_general(
        wm, do, tn, preferred_element_type=f32
    )

    @pl.when(n == 0)
    def _():
        tm_ref[...] = tm

    @pl.when(n != 0)
    def _():
        tm_ref[...] += tm


def attention_core(counts, targets, q, do, mk, got_kv):
    tokens, width = q.shape
    blocks = tokens // BLK
    mem = mk.shape[0]
    heads = width // HD
    nrows = NEAR * BLK
    qspec = pl.BlockSpec((BLK, HD), lambda h, n, c, t: (n, h))
    mspec = pl.BlockSpec((mem, HD), lambda h, n, c, t: (0, h))

    def kv_spec(j, which):
        return pl.BlockSpec((1, 1, BLK, HD), lambda h, n, c, t: (t[n * NEAR + j], which, 0, h))

    nspec = pl.BlockSpec((1, nrows, HD), lambda h, n, c, t: (n, 0, h))
    flops = 2 * tokens * width * (mem + nrows) * 4 + 2 * tokens * width * (nrows * 2 + mem * 2)
    grid_spec = pltpu.PrefetchScalarGridSpec(
        num_scalar_prefetch=2,
        grid=(heads, blocks),
        in_specs=[qspec, qspec, mspec]
        + [kv_spec(j, 0) for j in range(NEAR)]
        + [kv_spec(j, 1) for j in range(NEAR)],
        out_specs=[qspec, qspec, nspec, nspec, mspec],
    )
    return pl.pallas_call(
        _attn_body,
        grid_spec=grid_spec,
        out_shape=[
            jax.ShapeDtypeStruct((tokens, width), jnp.bfloat16),
            jax.ShapeDtypeStruct((tokens, width), jnp.bfloat16),
            jax.ShapeDtypeStruct((blocks, nrows, width), jnp.bfloat16),
            jax.ShapeDtypeStruct((blocks, nrows, width), jnp.bfloat16),
            jax.ShapeDtypeStruct((mem, width), jnp.float32),
        ],
        compiler_params=pltpu.CompilerParams(dimension_semantics=("arbitrary", "arbitrary")),
        cost_estimate=pl.CostEstimate(
            flops=flops,
            transcendentals=tokens * heads * (mem + nrows),
            bytes_accessed=2 * (4 * tokens * width + mem * width + 4 * blocks * nrows * width)
            + 4 * mem * width,
        ),
    )(counts, targets, q, do, mk, *([got_kv] * (2 * NEAR)))


def shards(
    queries,
    key_states,
    value_states,
    out_grad,
    memory,
    near_device,
    near_slot,
    near_count,
    writer_block,
):
    seq_devices = lax.axis_size("seq")
    batch_devices = lax.axis_size("batch")
    my_index = lax.axis_index("seq")
    tokens = queries.shape[1]
    row_width = queries.shape[2]
    near_width = near_device.shape[1]
    local_blocks = tokens // BLK
    entries = local_blocks * near_width
    rows_dev = MEM // seq_devices
    key_scaling_factor = 1.0 / math.sqrt(HD)
    block_scale = 1.0 / math.sqrt(BLK)
    value_blocks = value_states[0].reshape(local_blocks, BLK, row_width)
    key_blocks = key_states[0].reshape(local_blocks, BLK, row_width)

    target = near_device.reshape(seq_devices, entries)
    source_slot = near_slot.reshape(seq_devices, entries)
    my_target = lax.dynamic_index_in_dim(target, my_index, 0, keepdims=False)
    names_me = target == my_index
    send_idx = jnp.sum(jnp.where(names_me, source_slot, 0), axis=1)
    kv_blocks = jnp.stack([key_blocks, value_blocks], axis=1)
    send_kv = jnp.take(kv_blocks, send_idx, axis=0)
    got_kv = lax.all_to_all(send_kv, "seq", split_axis=0, concat_axis=0, tiled=True)

    value_sums = jnp.sum(value_blocks, axis=1, dtype=jnp.float32)
    all_sums = lax.all_to_all(
        jnp.broadcast_to(value_sums[None], (seq_devices, local_blocks, row_width)),
        "seq",
        split_axis=0,
        concat_axis=0,
        tiled=True,
    ).reshape(seq_devices * local_blocks, row_width)
    memory_keys = (memory + jnp.take(all_sums, writer_block, axis=0) * block_scale).astype(
        jnp.bfloat16
    )

    my_count = lax.dynamic_slice_in_dim(near_count, my_index * local_blocks, local_blocks, 0)
    attended_rows, query_rows_grad, key_part, value_part, term = attention_core(
        my_count, my_target, queries[0], out_grad[0], memory_keys, got_kv
    )
    key_part = key_part.reshape(entries, BLK, row_width)
    value_part = value_part.reshape(entries, BLK, row_width)
    term = term.reshape(seq_devices, rows_dev, row_width).astype(jnp.bfloat16)

    hits = my_target[None, :] == jnp.arange(seq_devices)[:, None]
    inverse = jnp.sum(jnp.where(hits, jnp.arange(entries)[None, :], 0), axis=1)
    back_keys = jnp.take(key_part, inverse, axis=0)
    back_values = jnp.take(value_part, inverse, axis=0)
    back = jnp.concatenate([back_keys, back_values, term], axis=1)
    got_back = lax.all_to_all(back, "seq", split_axis=0, concat_axis=0, tiled=True)
    select = jnp.sum(
        jnp.where(
            names_me[:, :, None],
            (source_slot[:, :, None] == jnp.arange(local_blocks)[None, None, :]).astype(jnp.float32),
            0.0,
        ),
        axis=1,
    ).astype(jnp.bfloat16)
    key_sum = jnp.einsum(
        "dl,dtw->ltw", select, got_back[:, :BLK], preferred_element_type=jnp.float32
    )
    value_sum = jnp.einsum(
        "dl,dtw->ltw", select, got_back[:, BLK : 2 * BLK], preferred_element_type=jnp.float32
    )
    row_grads = jnp.sum(got_back[:, 2 * BLK :].astype(jnp.float32), axis=0)
    my_writers = (
        lax.dynamic_slice_in_dim(writer_block, my_index * rows_dev, rows_dev, 0)
        - my_index * local_blocks
    )
    writer_match = (my_writers[:, None] == jnp.arange(local_blocks)[None, :])[:, :, None]
    spread = jnp.sum(jnp.where(writer_match, row_grads[:, None, :], 0.0), axis=0) * block_scale
    all_rows = lax.all_to_all(
        jnp.broadcast_to(row_grads[None], (batch_devices, rows_dev, row_width)),
        "batch",
        split_axis=0,
        concat_axis=0,
        tiled=True,
    )
    memory_grad = jnp.sum(all_rows, axis=0)
    attended = attended_rows.reshape(1, tokens, row_width)
    query_grad = query_rows_grad.reshape(1, tokens, row_width)
    key_grad = key_sum.astype(jnp.bfloat16).reshape(1, tokens, row_width)
    value_grad = (value_sum + spread[:, None, :]).astype(jnp.bfloat16).reshape(1, tokens, row_width)
    return (attended, query_grad, key_grad, value_grad, memory_grad)


def solution(mesh):
    placed = (
        P("batch", "seq", None),
        P("batch", "seq", None),
        P("batch", "seq", None),
        P("batch", "seq", None),
        P(),
        P(),
        P(),
        P(),
        P(),
    )
    return jax.shard_map(
        shards,
        mesh=mesh,
        in_specs=placed,
        out_specs=(
            P("batch", "seq", None),
            P("batch", "seq", None),
            P("batch", "seq", None),
            P("batch", "seq", None),
            P("seq", None),
        ),
        check_vma=False,
    )
```

time: 708 us -> 621 us (0.88)
  local copies, waits for them, and re-layouts: 115 us -> 41.3 us
  matrix products: 63.1 us -> 21.7 us
  Pallas kernels: 0 us -> 33.7 us
  other arithmetic: 71.9 us -> 54.5 us
  waiting for transfers between devices: 412 us -> 429 us
    dot_general x12 -> x0, matrix products: 41.4 us -> none  [the longest x1 8.44 us: shards(): jnp.einsum('cqhd,ckhd->chqk', head_output_gradient, neighbour_value_rows,...]
    pallas_call x0 -> x1, Pallas kernels: none -> 33.7 us  [attention_core(): pl.pallas_call(_attn_body, grid_spec=grid_spec, out_shape=[jax.ShapeDtype...]
    reshape x5 -> x0, local copies, waits for them, and re-layouts: 19.6 us -> none  [the longest x1 7.34 us: shards(): key_part = key_part.reshape(entries, BLK, row_width)]
    convert_element_type x6 -> x0, local copies, waits for them, and re-layouts: 17.6 us -> none  [the longest x1 6.84 us: shards(): value_part = jnp.einsum('chqk,cqhd->ckhd', neighbour_attention_weight, he...]
    unnamed x56 -> x12, local copies, waits for them, and re-layouts: 14.5 us -> 0.19 us
    gather x3 -> x2, local copies, waits for them, and re-layouts: 24.9 us -> 14.4 us  [the longest x1 7.25 us: shards(): back_keys = jnp.take(key_part, inverse, axis=0)]
    all_to_all x1, waiting for transfers between devices: 225 us -> 235 us  [shards(): lax.all_to_all(back, 'seq', split_axis=0, concat_axis=0, tiled=True)]
    reduce_sum x1 -> x0, other arithmetic: 8.43 us -> none  [shards(): row_total = jnp.sum(exp_mem, axis=-1) + jnp.sum(exp_near, axis=-1)]
  transfers between devices with their start and end apart: 4 -> 4, of which waited for: 2 -> 2; matrix products, arithmetic and copies ran while one was open for 9% -> 8% of each run, Pallas kernels for 0% -> 0%
where the time goes in v2:
time: 621 us; the launch traced here: 614 us
  waiting for transfers between devices  429 us (69%)
  other arithmetic  54.5 us (9%)
  local copies, waits for them, and re-layouts  41.3 us (7%)
  Pallas kernels  33.7 us (5%)
  starting transfers between devices  32.7 us (5%)
  matrix products  21.7 us (3%)
    all_to_all x1, waiting for transfers between devices, shards(): lax.all_to_all(back, 'seq', split_axis=0, concat_axis=0, tiled=True)  235 us
    all_to_all x1, waiting for transfers between devices, shards(): lax.all_to_all(send_kv, 'seq', split_axis=0, concat_axis=0, tiled=True)  194 us
    pallas_call x1, Pallas kernels, attention_core(): pl.pallas_call(_attn_body, grid_spec=grid_spec, out_shape=[jax.ShapeDtype...  33.7 us
    concatenate x1, other arithmetic, shards(): back = jnp.concatenate([back_keys, back_values, term], axis=1)  14.3 us
    select_n x2, other arithmetic, shards(): send_kv = jnp.take(kv_blocks, send_idx, axis=0)  14.2 us
    dot_general x1, matrix products, shards(): jnp.einsum('dl,dtw->ltw', select, got_back[:, BLK:2 * BLK], preferred_ele...  12.6 us
  transfers between devices with their start and end apart: 4, of which 2 were waited for; matrix products, arithmetic and copies ran while one was open for 8% of the time, Pallas kernels for 0%

profile of v2, /device:TPU:7, one launch (start us, length us, event | category | flops | bytes accessed | tf_op | source)
XLA Modules:
  0.0 613.8 jit_solution(5808193481711240535)
XLA Ops:
  0.6 1.1 convert_reduce_fusion.1
  1.8 0.8 broadcast_in_dim.102
  2.5 8.7 %all-to-all-start = ((f32[32,2,1024]{2,1,0:T(2,128)}), f32[32,2,1024]{2,1,0:T(2,128)S(1)}, u32[]{:S(2)}, u32[]{:S(2)}) async-start(f32[32,2,1024]{2,1,0:T(2,128)} %broadcast_in_dim.102), calls=%async_computation | async-start | bytes 524288 | tf_op jit(solution)/shard_map/all_to_all | solution.py:148
  11.2 0.7 select_reduce_fusion.3
  12.0 0.1 reduce_sum.74
  12.1 0.1 reduce_sum.75
  12.2 1.3 pad_maximum_fusion.1
  13.5 7.1 %gather_fusion.1 = bf16[32,2,128,1024]{3,2,1,0:T(8,128)(2,1)} fusion(bf16[2,2,128,1024]{3,2,0,1:T(8,128)(2,1)S(1)} %pad_maximum_fusion.1, s32[1024]{0:T(1024)S(1)} %pad_clamp_fusion.1), kind=kCustom, calls=%fused_computation.3 | custom fusion | bytes 33554560 | tf_op jit(solution)/shard_map/jit(_take)/gather | solution.py:144
  20.6 14.2 %broadcast_select_fusion = bf16[32,2,128,1024]{3,2,1,0:T(8,128)(2,1)} fusion(bf16[32,2,128,1024]{3,2,1,0:T(8,128)(2,1)} %gather_fusion.1, pred[32]{0:T(512)(128)(4,1)S(1)} %compare_and_fusion.2), kind=kLoop, calls=%fused_computation.5 | loop fusion | flops 8388608 | bytes 33554464 | tf_op jit(solution)/shard_map/jit(_take)/select_n | solution.py:144
  34.8 0.0 all-to-all-done
  34.8 7.5 %all-to-all-start.1 = ((bf16[32,2,128,1024]{3,2,1,0:T(8,128)(2,1)}), bf16[32,2,128,1024]{3,2,1,0:T(8,128)(2,1)}, u32[]{:S(2)}, u32[]{:S(2)}) async-start(bf16[32,2,128,1024]{3,2,1,0:T(8,128)(2,1)} %broadcast_select_fusion), calls=%async_computation.1 | async-start | bytes 33554432 | tf_op jit(solution)/shard_map/all_to_all | solution.py:145
  42.4 0.0 copy-done.1
  42.4 0.1 copy.28
  42.5 0.1 reshape.101
  42.5 0.0 copy-done.4
  42.5 0.6 dynamic_slice.10.cnt_ref
  43.1 0.1 select_reduce_fusion.2
  43.2 0.0 copy-done
  43.3 0.2 reshape.102
  43.5 5.4 gather_fusion
  48.9 0.0 copy-done.3
  48.9 5.4 add_convert_fusion.mk_ref
  54.3 194.3 %all-to-all-done.1.rest_0_.rest_1_.rest_2_.rest_3_.rest_4_.rest_5_.rest_6_.rest_7_.rest_8_.rest_9_.rest_10_.rest_11_.rest_12_.rest_13_.rest_14_.rest_15_ = bf16[32,2,128,1024]{3,2,1,0:T(8,128)(2,1)} async-done(((bf16[32,2,128,1024]{3,2,1,0:T(8,128)(2,1)}), bf16[32,2,128,1024]{3,2,1,0:T(8,128)(2,1)}, u32[]{:S(2)}, u32[]{:S(2)}) %all-to-all-start.1) | async-done | bytes 16777248 | tf_op jit(solution)/shard_map/all_to_all | solution.py:145
  248.6 33.7 %shard_map.128 = (bf16[256,1024]{1,0:T(8,128)(2,1)}, bf16[256,1024]{1,0:T(8,128)(2,1)}, bf16[2,1024,1024]{2,1,0:T(8,128)(2,1)}, bf16[2,1024,1024]{2,1,0:T(8,128)(2,1)}, f32[1024,1024]{1,0:T(8,128)}) custom-call(s32[2]{0:T(128)} %dynamic_slice.10.cnt_ref, s32[16]{0:T(128)} %copy-done.3, bf16[256,1024]{1,0:T(8,128)(2,1)} %bitcast.29, ...), custom_call_target="tpu_custom_call" | custom-call | flops 6442450944 | bytes 25165824 | tf_op jit(solution)/shard_map/pallas_call | solution.py:93
  282.3 2.5 convert_element_type.39
  284.8 7.3 %gather_fusion.2 = bf16[32,128,1024]{2,1,0:T(8,128)(2,1)} fusion(bf16[16,128,1024]{2,1,0:T(8,128)(2,1)} %bitcast.25, s32[1024]{0:T(1024)S(1)} %pad_clamp_fusion), kind=kCustom, calls=%fused_computation.clone | custom fusion | bytes 16777344 | tf_op jit(solution)/shard_map/jit(_take)/gather | solution.py:169
  292.1 7.1 %gather_fusion.3 = bf16[32,128,1024]{2,1,0:T(8,128)(2,1)} fusion(bf16[16,128,1024]{2,1,0:T(8,128)(2,1)} %bitcast.24, s32[1024]{0:T(1024)S(1)} %pad_clamp_fusion), kind=kCustom, calls=%fused_computation.1.clone | custom fusion | bytes 16777344 | tf_op jit(solution)/shard_map/jit(_take)/gather | solution.py:170
  299.2 11.8 %broadcast_select_fusion.2 = (bf16[32,128,1024]{2,1,0:T(8,128)(2,1)}, bf16[32,128,1024]{2,1,0:T(8,128)(2,1)}) fusion(bf16[32,128,1024]{2,1,0:T(8,128)(2,1)} %gather_fusion.2, pred[32]{0:T(512)(128)(4,1)S(1)} %compare_and_fusion.1, bf16[32,128,1024]{2,1,0:T(8,128)(2,1)} %gather_fusion.3), kind=kLoop, calls=%fused_computation.11 | loop fusion | flops 8388608 | bytes 33554464 | tf_op jit(solution)/shard_map/jit(_take)/select_n | solution.py:169
  311.0 14.3 %pad_maximum_fusion = bf16[32,288,1024]{2,1,0:T(8,128)(2,1)} fusion(bf16[32,32,1024]{2,1,0:T(8,128)(2,1)S(1)} %bitcast.26, bf16[32,128,1024]{2,1,0:T(8,128)(2,1)} %get-tuple-element.19, bf16[32,128,1024]{2,1,0:T(8,128)(2,1)} %get-tuple-element.18), kind=kLoop, calls=%fused_computation.4 | loop fusion | flops 56623104 | bytes 37748736 | tf_op jit(solution)/shard_map/concatenate | solution.py:171
  325.3 12.3 %all-to-all-start.2 = ((bf16[32,288,1024]{2,1,0:T(8,128)(2,1)}), bf16[32,288,1024]{2,1,0:T(8,128)(2,1)}, u32[]{:S(2)}, u32[]{:S(2)}) async-start(bf16[32,288,1024]{2,1,0:T(8,128)(2,1)} %pad_maximum_fusion), calls=%async_computation.2 | async-start | bytes 37748736 | tf_op jit(solution)/shard_map/all_to_all | solution.py:172
  337.6 0.0 copy-done.2
  337.6 0.1 copy.30
  337.7 0.1 copy.29
  337.8 0.1 eq.64
  337.9 0.1 copy.31
  338.0 0.1 dynamic-slice_subtract_fusion
  338.1 234.8 %all-to-all-done.2 = bf16[32,288,1024]{2,1,0:T(8,128)(2,1)} async-done(((bf16[32,288,1024]{2,1,0:T(8,128)(2,1)}), bf16[32,288,1024]{2,1,0:T(8,128)(2,1)}, u32[]{:S(2)}, u32[]{:S(2)}) %all-to-all-start.2) | async-done | bytes 18874400 | tf_op jit(solution)/shard_map/all_to_all | solution.py:172
  572.9 2.0 convert_reduce_fusion
  574.8 0.1 select_reduce_fusion
  575.0 9.5 %fusion.19 = (bf16[32,128,1024]{2,1,0:T(8,128)(2,1)}, bf16[32,128,1024]{2,1,0:T(8,128)(2,1)S(1)}) fusion(bf16[32,288,1024]{2,1,0:T(8,128)(2,1)} %all-to-all-done.2), kind=kLoop, calls=%fused_computation.45 | loop fusion | bytes 33554432 | tf_op jit(solution)/shard_map/slice | solution.py:185
  584.5 9.1 %fusion.4 = bf16[2,128,1024]{2,0,1:T(2,128)(2,1)S(1)} fusion(bf16[32,128,1024]{2,1,0:T(8,128)(2,1)S(1)} %get-tuple-element.17, bf16[32,2]{0,1:T(2,128)(2,1)S(1)} %select_reduce_fusion.1), kind=kOutput, calls=%fused_computation.14 | convolution fusion | flops 17039360 | bytes 8913024 | tf_op jit(solution)/shard_map/dl,dtw->ltw/dot_general | solution.py:181
  593.6 0.9 copy.33
  594.5 0.9 broadcast_in_dim.115
  595.4 4.2 all-to-all-start.3
  599.6 12.6 %fusion.10 = bf16[2,128,1024]{2,0,1:T(2,128)(2,1)S(1)} fusion(bf16[32,128,1024]{2,1,0:T(8,128)(2,1)} %get-tuple-element.16, f32[2,1024]{1,0:T(2,128)S(1)} %broadcast_multiply_fusion, bf16[32,2]{0,1:T(2,128)(2,1)S(1)} %select_reduce_fusion.1), kind=kOutput, calls=%fused_computation.16 | convolution fusion | flops 17301504 | bytes 8921216 | tf_op jit(solution)/shard_map/dl,dtw->ltw/dot_general | solution.py:184
  612.2 0.9 copy.35
  613.1 0.0 all-to-all-done.3
  613.1 0.7 reduce_sum.81
  (18 shorter events, 0.1 us)
Async XLA Ops:
  2.5 32.3 %all-to-all-start = ((f32[32,2,1024]{2,1,0:T(2,128)}), f32[32,2,1024]{2,1,0:T(2,128)S(1)}, u32[]{:S(2)}, u32[]{:S(2)}) async-start(f32[32,2,1024]{2,1,0:T(2,128)} %broadcast_in_dim.102), calls=%async_computation | async-start | bytes 524288 | tf_op jit(solution)/shard_map/all_to_all | solution.py:148
  34.8 7.5 %copy-start.1 = (s32[64,8]{0,1:T(8,128)S(1)}, s32[64,8]{0,1:T(8,128)}, u32[]{:S(2)}) copy-start(s32[64,8]{0,1:T(8,128)} %param.16) | copy-start | bytes 6148
  34.8 7.7 %copy-start.4 = (s32[64]{0:T(128)S(1)}, s32[64]{0:T(128)}, u32[]{:S(2)}) copy-start(s32[64]{0:T(128)} %param.18) | copy-start | bytes 772
  34.8 8.4 %copy-start = (s32[1024]{0:T(1024)S(1)}, s32[1024]{0:T(1024)}, u32[]{:S(2)}) copy-start(s32[1024]{0:T(1024)} %param.19) | copy-start | bytes 12292
  34.8 213.7 %all-to-all-start.1 = ((bf16[32,2,128,1024]{3,2,1,0:T(8,128)(2,1)}), bf16[32,2,128,1024]{3,2,1,0:T(8,128)(2,1)}, u32[]{:S(2)}, u32[]{:S(2)}) async-start(bf16[32,2,128,1024]{3,2,1,0:T(8,128)(2,1)} %broadcast_select_fusion), calls=%async_computation.1 | async-start | bytes 33554432 | tf_op jit(solution)/shard_map/all_to_all | solution.py:145
  43.1 5.8 copy-start.3
  325.3 12.3 %copy-start.2 = (s32[64,8]{0,1:T(8,128)S(1)}, s32[64,8]{0,1:T(8,128)}, u32[]{:S(2)}) copy-start(s32[64,8]{0,1:T(8,128)} %param.17) | copy-start | bytes 6148
  325.3 247.5 %all-to-all-start.2 = ((bf16[32,288,1024]{2,1,0:T(8,128)(2,1)}), bf16[32,288,1024]{2,1,0:T(8,128)(2,1)}, u32[]{:S(2)}, u32[]{:S(2)}) async-start(bf16[32,288,1024]{2,1,0:T(8,128)(2,1)} %pad_maximum_fusion), calls=%async_computation.2 | async-start | bytes 37748736 | tf_op jit(solution)/shard_map/all_to_all | solution.py:172
  595.4 17.7 %all-to-all-start.3 = ((f32[4,32,1024]{2,1,0:T(8,128)}), f32[4,32,1024]{2,1,0:T(8,128)S(1)}, u32[]{:S(2)}, u32[]{:S(2)}) async-start(f32[4,32,1024]{2,1,0:T(8,128)} %broadcast_in_dim.115), calls=%async_computation.3 | async-start | bytes 1048576 | tf_op jit(solution)/shard_map/all_to_all | solution.py:194

commit v3 on v2

v3 whole, which is shorter than its diff:
```python
import math

import jax
import jax.numpy as jnp
from jax import lax
from jax.experimental import pallas as pl
from jax.experimental.pallas import tpu as pltpu
from jax.sharding import PartitionSpec as P

HEADS = 8
HD = 128
BLK = 128
MEM = 1024
NEAR = 8


def _attn_body(cnt_ref, nb_ref, q_ref, do_ref, mk_ref, *rest):
    k_refs = rest[:NEAR]
    v_refs = rest[NEAR : 2 * NEAR]
    _, o_ref, dq_ref, tm_ref, dkv_hbm, dks, dvs, sems = rest[2 * NEAR :]
    h = pl.program_id(0)
    n = pl.program_id(1)
    blocks = pl.num_programs(1)
    steps = pl.num_programs(0) * blocks
    step = h * blocks + n
    slot = step % 2
    heads = pl.num_programs(0)
    scale = 1.0 / math.sqrt(HD)
    f32 = jnp.float32
    nt = (((1,), (1,)), ((), ()))
    tn = (((0,), (0,)), ((), ()))
    q = q_ref[...]
    do = do_ref[...]
    mk = mk_ref[...]
    nk = jnp.concatenate([r[...] for r in k_refs], axis=0)
    nv = jnp.concatenate([r[...] for r in v_refs], axis=0)
    sm = lax.dot_general(q, mk, nt, preferred_element_type=f32) * scale
    sn = lax.dot_general(q, nk, nt, preferred_element_type=f32) * scale
    col = lax.broadcasted_iota(jnp.int32, sn.shape, 1) // BLK
    sn = jnp.where(col < cnt_ref[n], sn, -jnp.inf)
    m = jnp.maximum(jnp.max(sm, axis=1, keepdims=True), jnp.max(sn, axis=1, keepdims=True))
    em = jnp.exp(sm - m)
    en = jnp.exp(sn - m)
    total = jnp.sum(em, axis=1, keepdims=True) + jnp.sum(en, axis=1, keepdims=True)
    pm = em / total
    pn = en / total
    wm = pm.astype(jnp.bfloat16)
    wn = pn.astype(jnp.bfloat16)
    o = (
        jnp.dot(wm, mk, preferred_element_type=f32) + jnp.dot(wn, nv, preferred_element_type=f32)
    ).astype(jnp.bfloat16)
    o_ref[...] = o
    gd = jnp.sum(do.astype(f32) * o.astype(f32), axis=1, keepdims=True)
    dpm = lax.dot_general(do, mk, nt, preferred_element_type=f32)
    dpn = lax.dot_general(do, nv, nt, preferred_element_type=f32)
    dsm = (pm * (dpm - gd)).astype(jnp.bfloat16)
    dsn = (pn * (dpn - gd)).astype(jnp.bfloat16)
    dq_ref[...] = (
        (jnp.dot(dsm, mk, preferred_element_type=f32) + jnp.dot(dsn, nk, preferred_element_type=f32))
        * scale
    ).astype(jnp.bfloat16)
    dk = (lax.dot_general(dsn, q, tn, preferred_element_type=f32) * scale).astype(jnp.bfloat16)
    dv = lax.dot_general(wn, do, tn, preferred_element_type=f32).astype(jnp.bfloat16)
    tm = lax.dot_general(dsm, q, tn, preferred_element_type=f32) * scale + lax.dot_general(
        wm, do, tn, preferred_element_type=f32
    )

    @pl.when(n == 0)
    def _():
        tm_ref[...] = tm

    @pl.when(n != 0)
    def _():
        tm_ref[...] += tm

    def copies(at_step, at_slot):
        at_h = at_step // blocks
        at_n = at_step % blocks
        out = []
        for j in range(NEAR):
            rows = pl.ds(pl.multiple_of(nb_ref[at_n * NEAR + j] * BLK, BLK), BLK)
            out.append(
                pltpu.make_async_copy(
                    dks.at[at_slot, j],
                    dkv_hbm.at[rows, pl.ds(pl.multiple_of(at_h * HD, HD), HD)],
                    sems.at[at_slot, j],
                )
            )
            out.append(
                pltpu.make_async_copy(
                    dvs.at[at_slot, j],
                    dkv_hbm.at[rows, pl.ds(pl.multiple_of((heads + at_h) * HD, HD), HD)],
                    sems.at[at_slot, NEAR + j],
                )
            )
        return out

    @pl.when(step >= 2)
    def _():
        for c in copies(step - 2, slot):
            c.wait()

    for j in range(NEAR):
        dks[slot, j] = dk[j * BLK : (j + 1) * BLK]
        dvs[slot, j] = dv[j * BLK : (j + 1) * BLK]
    for c in copies(step, slot):
        c.start()

    @pl.when(step == steps - 1)
    def _():
        for c in copies(step - 1, 1 - slot):
            c.wait()
        for c in copies(step, slot):
            c.wait()


def attention_core(counts, near_rows, q, do, mk, kv_all):
    tokens, width = q.shape
    blocks = tokens // BLK
    mem = mk.shape[0]
    heads = width // HD
    nrows = NEAR * BLK
    qspec = pl.BlockSpec((BLK, HD), lambda h, n, c, t: (n, h))
    mspec = pl.BlockSpec((mem, HD), lambda h, n, c, t: (0, h))

    def kv_spec(j, which):
        return pl.BlockSpec((BLK, HD), lambda h, n, c, t: (t[n * NEAR + j], which * heads + h))

    anyspec = pl.BlockSpec(memory_space=pl.ANY)
    flops = 2 * tokens * width * (mem + nrows) * 4 + 2 * tokens * width * (nrows * 2 + mem * 2)
    grid_spec = pltpu.PrefetchScalarGridSpec(
        num_scalar_prefetch=2,
        grid=(heads, blocks),
        in_specs=[qspec, qspec, mspec]
        + [kv_spec(j, 0) for j in range(NEAR)]
        + [kv_spec(j, 1) for j in range(NEAR)]
        + [anyspec],
        out_specs=[qspec, qspec, mspec, anyspec],
        scratch_shapes=[
            pltpu.VMEM((2, NEAR, BLK, HD), jnp.bfloat16),
            pltpu.VMEM((2, NEAR, BLK, HD), jnp.bfloat16),
            pltpu.SemaphoreType.DMA((2, 2 * NEAR)),
        ],
    )
    zeros = jnp.zeros(kv_all.shape, jnp.bfloat16)
    return pl.pallas_call(
        _attn_body,
        grid_spec=grid_spec,
        out_shape=[
            jax.ShapeDtypeStruct((tokens, width), jnp.bfloat16),
            jax.ShapeDtypeStruct((tokens, width), jnp.bfloat16),
            jax.ShapeDtypeStruct((mem, width), jnp.float32),
            jax.ShapeDtypeStruct(kv_all.shape, jnp.bfloat16),
        ],
        input_output_aliases={2 + 3 + 2 * NEAR: 3},
        compiler_params=pltpu.CompilerParams(dimension_semantics=("arbitrary", "arbitrary")),
        cost_estimate=pl.CostEstimate(
            flops=flops,
            transcendentals=tokens * heads * (mem + nrows),
            bytes_accessed=2 * (4 * tokens * width + mem * width + 4 * blocks * nrows * width)
            + 4 * mem * width,
        ),
    )(counts, near_rows, q, do, mk, *([kv_all] * (2 * NEAR)), zeros)


def shards(
    queries,
    key_states,
    value_states,
    out_grad,
    memory,
    near_device,
    near_slot,
    near_count,
    writer_block,
):
    seq_devices = lax.axis_size("seq")
    batch_devices = lax.axis_size("batch")
    my_index = lax.axis_index("seq")
    tokens = queries.shape[1]
    row_width = queries.shape[2]
    local_blocks = tokens // BLK
    rows_dev = MEM // seq_devices
    block_scale = 1.0 / math.sqrt(BLK)
    value_blocks = value_states[0].reshape(local_blocks, BLK, row_width)

    kv_all = lax.all_gather(
        jnp.concatenate([key_states[0], value_states[0]], axis=-1), "seq", axis=0, tiled=True
    )

    value_sums = jnp.sum(value_blocks, axis=1, dtype=jnp.float32)
    all_sums = lax.all_to_all(
        jnp.broadcast_to(value_sums[None], (seq_devices, local_blocks, row_width)),
        "seq",
        split_axis=0,
        concat_axis=0,
        tiled=True,
    ).reshape(seq_devices * local_blocks, row_width)
    memory_keys = (memory + jnp.take(all_sums, writer_block, axis=0) * block_scale).astype(
        jnp.bfloat16
    )
    near_block = (near_device * local_blocks + near_slot).astype(jnp.int32)
    my_near = lax.dynamic_slice_in_dim(near_block, my_index * local_blocks, local_blocks, 0).reshape(-1)
    my_count = lax.dynamic_slice_in_dim(near_count, my_index * local_blocks, local_blocks, 0)
    attended_rows, query_rows_grad, term, dkv = attention_core(
        my_count, my_near, queries[0], out_grad[0], memory_keys, kv_all
    )
    kv_grad = lax.psum_scatter(dkv, "seq", scatter_dimension=0, tiled=True)
    row_grads = lax.psum_scatter(
        term.astype(jnp.bfloat16), "seq", scatter_dimension=0, tiled=True
    ).astype(jnp.float32)
    my_writers = (
        lax.dynamic_slice_in_dim(writer_block, my_index * rows_dev, rows_dev, 0)
        - my_index * local_blocks
    )
    writer_match = (my_writers[:, None] == jnp.arange(local_blocks)[None, :])[:, :, None]
    spread = jnp.sum(jnp.where(writer_match, row_grads[:, None, :], 0.0), axis=0) * block_scale
    all_rows = lax.all_to_all(
        jnp.broadcast_to(row_grads[None], (batch_devices, rows_dev, row_width)),
        "batch",
        split_axis=0,
        concat_axis=0,
        tiled=True,
    )
    memory_grad = jnp.sum(all_rows, axis=0)
    value_sum = kv_grad[:, row_width:].astype(jnp.float32).reshape(local_blocks, BLK, row_width)
    attended = attended_rows.reshape(1, tokens, row_width)
    query_grad = query_rows_grad.reshape(1, tokens, row_width)
    key_grad = kv_grad[:, :row_width].reshape(1, tokens, row_width)
    value_grad = (value_sum + spread[:, None, :]).astype(jnp.bfloat16).reshape(1, tokens, row_width)
    return (attended, query_grad, key_grad, value_grad, memory_grad)


def solution(mesh):
    placed = (
        P("batch", "seq", None),
        P("batch", "seq", None),
        P("batch", "seq", None),
        P("batch", "seq", None),
        P(),
        P(),
        P(),
        P(),
        P(),
    )
    return jax.shard_map(
        shards,
        mesh=mesh,
        in_specs=placed,
        out_specs=(
            P("batch", "seq", None),
            P("batch", "seq", None),
            P("batch", "seq", None),
            P("batch", "seq", None),
            P("seq", None),
        ),
        check_vma=False,
    )
```

time: 621 us -> 437 us (0.70)
  waiting for transfers between devices: 429 us -> 332 us
  other arithmetic: 54.5 us -> 17.2 us
  matrix products: 21.7 us -> 0 us
  starting transfers between devices: 32.7 us -> 12.8 us
  local copies, waits for them, and re-layouts: 41.3 us -> 22.3 us
  between operations: 0.81 us -> 13.9 us
    all_to_all x2 -> x0, waiting for transfers between devices: 429 us -> none  [the longest x1 235 us: shards(): lax.all_to_all(back, 'seq', split_axis=0, concat_axis=0, tiled=True)]
    reduce_scatter x0 -> x2, waiting for transfers between devices: none -> 231 us  [the longest x1 158 us: shards(): kv_grad = lax.psum_scatter(dkv, 'seq', scatter_dimension=0, tiled=True)]
    all_gather x0 -> x1, waiting for transfers between devices: none -> 88.1 us  [shards(): lax.all_gather(jnp.concatenate([key_states[0], value_states[0]], axis=-1)...]
    select_n x4 -> x0, other arithmetic: 26 us -> none  [the longest x2 14.2 us: shards(): send_kv = jnp.take(kv_blocks, send_idx, axis=0)]
    dot_general x2 -> x0, matrix products: 21.7 us -> none  [the longest x1 12.6 us: shards(): jnp.einsum('dl,dtw->ltw', select, got_back[:, BLK:2 * BLK], preferred_ele...]
    gather x3 -> x0, local copies, waits for them, and re-layouts: 21.5 us -> none  [the longest x1 7.25 us: shards(): back_keys = jnp.take(key_part, inverse, axis=0)]
    all_to_all x2 -> x0, starting transfers between devices: 19.8 us -> none  [the longest x1 12.3 us: shards(): lax.all_to_all(back, 'seq', split_axis=0, concat_axis=0, tiled=True)]
    concatenate x1, other arithmetic: 14.3 us -> 2.26 us  [shards(): jnp.concatenate([key_states[0], value_states[0]], axis=-1)]
  transfers between devices with their start and end apart: 4 -> 5, of which waited for: 2 -> 5; matrix products, arithmetic and copies ran while one was open for 8% -> 4% of each run, Pallas kernels for 0% -> 0%
where the time goes in v3:
time: 437 us; the launch traced here: 435 us
  waiting for transfers between devices  332 us (76%)
  Pallas kernels  37.1 us (8%)
  local copies, waits for them, and re-layouts  22.3 us (5%)
  other arithmetic  17.2 us (4%)
  between operations  13.9 us (3%)
  starting transfers between devices  12.8 us (3%)
    reduce_scatter x1, waiting for transfers between devices, shards(): kv_grad = lax.psum_scatter(dkv, 'seq', scatter_dimension=0, tiled=True)  158 us
    all_gather x1, waiting for transfers between devices, shards(): lax.all_gather(jnp.concatenate([key_states[0], value_states[0]], axis=-1)...  88.1 us
    reduce_scatter x1, waiting for transfers between devices, shards(): lax.psum_scatter(term.astype(jnp.bfloat16), 'seq', scatter_dimension=0, t...  73.8 us
    pallas_call x1, Pallas kernels, attention_core(): pl.pallas_call(_attn_body, grid_spec=grid_spec, out_shape=[jax.ShapeDtype...  37.1 us
    broadcast_in_dim x1, local copies, waits for them, and re-layouts, attention_core(): zeros = jnp.zeros(kv_all.shape, jnp.bfloat16)  11 us
  transfers between devices with their start and end apart: 5, of which 5 were waited for; matrix products, arithmetic and copies ran while one was open for 4% of the time, Pallas kernels for 0%

profile of v3, /device:TPU:7, one launch (start us, length us, event | category | flops | bytes accessed | tf_op | source)
XLA Modules:
  0.0 435.4 jit_solution(5762515778631000760)
XLA Ops:
  7.2 0.0 copy-start
  7.2 0.0 copy-start.1
  7.2 0.0 copy-start.2
  7.2 0.0 copy-start.3
  7.2 0.0 all-gather.2.cloned.1.call-start
  7.3 2.3 pad_maximum_fusion
  9.5 0.0 all-gather.2.cloned.1.call-update
  9.5 1.1 convert_reduce_fusion
  10.7 0.8 broadcast_in_dim.53
  11.5 8.7 %all-to-all-start = ((f32[32,2,1024]{2,1,0:T(2,128)}), f32[32,2,1024]{2,1,0:T(2,128)S(1)}, u32[]{:S(2)}, u32[]{:S(2)}) async-start(f32[32,2,1024]{2,1,0:T(2,128)} %broadcast_in_dim.53), calls=%async_computation | async-start | bytes 524288 | tf_op jit(solution)/shard_map/all_to_all | solution.py:192
  20.1 0.0 reduce-scatter.5.cloned.1.call-start
  20.2 0.0 copy-done
  20.2 0.0 copy-done.1
  20.2 0.0 copy-done.2
  20.3 0.1 constant_dynamic-slice_fusion
  20.3 0.0 copy-done.3
  20.3 0.6 dynamic_slice.9.cnt_ref
  20.9 0.1 copy.16
  21.0 0.6 reshape.68.nb_ref
  21.6 6.0 %all-to-all-done = f32[32,2,1024]{2,1,0:T(2,128)S(1)} async-done(((f32[32,2,1024]{2,1,0:T(2,128)}), f32[32,2,1024]{2,1,0:T(2,128)S(1)}, u32[]{:S(2)}, u32[]{:S(2)}) %all-to-all-start) | async-done | bytes 262176 | tf_op jit(solution)/shard_map/all_to_all | solution.py:192
  27.6 0.2 reshape.69
  27.8 5.4 %gather_fusion = f32[1024,1024]{1,0:T(8,128)} fusion(f32[64,1024]{1,0:T(8,128)S(1)} %reshape.69, s32[1024]{0:T(1024)S(1)} %fusion.1), kind=kCustom, calls=%fused_computation | custom fusion | bytes 8392704 | tf_op jit(solution)/shard_map/jit(_take)/gather | solution.py:199
  33.2 5.6 %add_convert_fusion.mk_ref = bf16[1024,1024]{1,0:T(8,128)(2,1)} fusion(f32[1024,1024]{1,0:T(8,128)} %param.13, f32[1024,1024]{1,0:T(8,128)} %gather_fusion, pred[1024]{0:T(1024)(128)(4,1)S(1)} %compare_and_fusion), kind=kLoop, calls=%fused_computation.1 | loop fusion | flops 4194304 | bytes 10486784 | tf_op jit(solution)/shard_map/convert_element_type | solution.py:199
  38.8 88.1 %all-gather.2.cloned.1.call-done.rest_0_.rest_1_.rest_2_.rest_3_.rest_4_.rest_5_.rest_6_.rest_7_.rest_8_.rest_9_.rest_10_.rest_11_.rest_12_.rest_13_.rest_14_.rest_15_ = bf16[8192,2048]{1,0:T(8,128)(2,1)} async-done(((bf16[256,2048]{1,0:T(8,128)(2,1)}), bf16[8192,2048]{1,0:T(8,128)(2,1)}) %all-gather.2.cloned.1.call-update) | async-done | bytes 33554448 | tf_op jit(solution)/shard_map/all_gather | solution.py:187
  126.9 11.0 %broadcast_in_dim.56.rest_16_ = bf16[8192,2048]{1,0:T(8,128)(2,1)} broadcast(bf16[]{:T(256)} %constant.8.clone.1), dimensions={} | broadcast | bytes 33554432 | tf_op jit(solution)/shard_map/broadcast_in_dim | solution.py:145
  137.8 37.1 %shard_map.128 = (bf16[256,1024]{1,0:T(8,128)(2,1)}, bf16[256,1024]{1,0:T(8,128)(2,1)}, f32[1024,1024]{1,0:T(8,128)}, bf16[8192,2048]{1,0:T(8,128)(2,1)}) custom-call(s32[2]{0:T(128)} %dynamic_slice.9.cnt_ref, s32[16]{0:T(128)} %reshape.68.nb_ref, bf16[256,1024]{1,0:T(8,128)(2,1)} %bitcast.19, ...), custom_call_target="tpu_custom_call", output_to_operand_aliasing={{3}: (21, {})} | custom-call | flops 6442450944 | bytes 25165824 | tf_op jit(solution)/shard_map/pallas_call | solution.py:146
  174.9 3.8 convert_element_type.33
  178.8 0.0 reduce-scatter.5.cloned.1.call-update
  178.8 0.0 reduce-scatter.3.cloned.1.call-start
  178.8 0.7 reduce-scatter.3.cloned.1.call-update
  179.5 0.8 dynamic-slice_subtract_fusion
  180.3 73.8 %reduce-scatter.5.cloned.1.call-done = bf16[32,1024]{1,0:T(8,128)(2,1)} async-done(((bf16[1024,1024]{1,0:T(8,128)(2,1)}), bf16[32,1024]{1,0:T(8,128)(2,1)}) %reduce-scatter.5.cloned.1.call-update) | async-done | bytes 65552 | tf_op jit(solution)/shard_map/reduce_scatter | solution.py:209
  254.1 1.7 broadcast_in_dim.60
  255.8 4.0 all-to-all-start.1
  259.8 0.8 convert_element_type.34
  260.7 0.1 select_reduce_fusion
  260.8 5.9 %all-to-all-done.1 = f32[4,32,1024]{2,1,0:T(8,128)S(1)} async-done(((f32[4,32,1024]{2,1,0:T(8,128)}), f32[4,32,1024]{2,1,0:T(8,128)S(1)}, u32[]{:S(2)}, u32[]{:S(2)}) %all-to-all-start.1) | async-done | bytes 524320 | tf_op jit(solution)/shard_map/all_to_all | solution.py:218
  266.8 0.7 reduce_sum.29
  267.4 157.6 %reduce-scatter.3.cloned.1.call-done = bf16[256,2048]{1,0:T(8,128)(2,1)} async-done(((bf16[8192,2048]{1,0:T(8,128)(2,1)}), bf16[256,2048]{1,0:T(8,128)(2,1)}) %reduce-scatter.3.cloned.1.call-update) | async-done | bytes 1048592 | tf_op jit(solution)/shard_map/reduce_scatter | solution.py:208
  425.0 1.9 slice_bitcast_fusion
  426.9 2.0 fusion
  (5 shorter events, 0.0 us)
Async XLA Ops:
  7.2 13.0 %copy-start = (s32[1024]{0:T(1024)S(1)}, s32[1024]{0:T(1024)}, u32[]{:S(2)}) copy-start(s32[1024]{0:T(1024)} %param.17) | copy-start | bytes 12292
  7.2 13.0 %copy-start.1 = (s32[64,8]{0,1:T(8,128)S(1)}, s32[64,8]{0,1:T(8,128)}, u32[]{:S(2)}) copy-start(s32[64,8]{0,1:T(8,128)} %param.15) | copy-start | bytes 6148
  7.2 13.0 %copy-start.2 = (s32[64,8]{0,1:T(8,128)S(1)}, s32[64,8]{0,1:T(8,128)}, u32[]{:S(2)}) copy-start(s32[64,8]{0,1:T(8,128)} %param.14) | copy-start | bytes 6148
  7.2 13.1 %copy-start.3 = (s32[64]{0:T(128)S(1)}, s32[64]{0:T(128)}, u32[]{:S(2)}) copy-start(s32[64]{0:T(128)} %param.16) | copy-start | bytes 772
  7.2 119.7 %all-gather.2.cloned.1.call-start = ((), (), s32[]{:S(2)}) async-start(), calls=%async_computation.4 | async-start | bytes 34603008 | tf_op jit(solution)/shard_map/all_gather | solution.py:187
  11.5 16.1 %all-to-all-start = ((f32[32,2,1024]{2,1,0:T(2,128)}), f32[32,2,1024]{2,1,0:T(2,128)S(1)}, u32[]{:S(2)}, u32[]{:S(2)}) async-start(f32[32,2,1024]{2,1,0:T(2,128)} %broadcast_in_dim.53), calls=%async_computation | async-start | bytes 524288 | tf_op jit(solution)/shard_map/all_to_all | solution.py:192
  20.1 234.0 %reduce-scatter.5.cloned.1.call-start = ((), (), s32[]{:S(2)}) async-start(), calls=%async_computation.6 | async-start | bytes 2162688 | tf_op jit(solution)/shard_map/reduce_scatter | solution.py:209
  178.8 246.2 %reduce-scatter.3.cloned.1.call-start = ((), (), s32[]{:S(2)}) async-start(), calls=%async_computation.5 | async-start | bytes 34603008 | tf_op jit(solution)/shard_map/reduce_scatter | solution.py:208
  255.8 10.9 %all-to-all-start.1 = ((f32[4,32,1024]{2,1,0:T(8,128)}), f32[4,32,1024]{2,1,0:T(8,128)S(1)}, u32[]{:S(2)}, u32[]{:S(2)}) async-start(f32[4,32,1024]{2,1,0:T(8,128)} %broadcast_in_dim.60), calls=%async_computation.3 | async-start | bytes 1048576 | tf_op jit(solution)/shard_map/all_to_all | solution.py:218
Sparse Core Ops, SparseCore 0:
  10.3 116.5 all-gather.1
  178.9 75.1 reduce-scatter.4
  258.0 166.9 reduce-scatter.2

commit v4 on v3

--- a/solution.py
+++ b/solution.py
@@ -14,10 +14,11 @@
 NEAR = 8
 
 
-def _attn_body(cnt_ref, nb_ref, q_ref, do_ref, mk_ref, *rest):
+def _attn_body(cnt_ref, nb_ref, free_ref, q_ref, do_ref, mk_ref, *rest):
     k_refs = rest[:NEAR]
     v_refs = rest[NEAR : 2 * NEAR]
-    _, o_ref, dq_ref, tm_ref, dkv_hbm, dks, dvs, sems = rest[2 * NEAR :]
+    o_ref, dq_ref, tm_ref, dkv_hbm, dks, dvs, sems, zero_strip, zero_sems = rest[2 * NEAR :]
+    unnamed = zero_sems.shape[0]
     h = pl.program_id(0)
     n = pl.program_id(1)
     blocks = pl.num_programs(1)
@@ -29,6 +30,22 @@
     f32 = jnp.float32
     nt = (((1,), (1,)), ((), ()))
     tn = (((0,), (0,)), ((), ()))
+    def zero_copies():
+        return [
+            pltpu.make_async_copy(
+                zero_strip,
+                dkv_hbm.at[pl.ds(pl.multiple_of(free_ref[i] * BLK, BLK), BLK)],
+                zero_sems.at[i],
+            )
+            for i in range(unnamed)
+        ]
+
+    @pl.when(step == 0)
+    def _():
+        zero_strip[...] = jnp.zeros(zero_strip.shape, zero_strip.dtype)
+        for c in zero_copies():
+            c.start()
+
     q = q_ref[...]
     do = do_ref[...]
     mk = mk_ref[...]
@@ -112,37 +129,39 @@
             c.wait()
         for c in copies(step, slot):
             c.wait()
-
-
-def attention_core(counts, near_rows, q, do, mk, kv_all):
+        for c in zero_copies():
+            c.wait()
+
+
+def attention_core(counts, near_rows, free_rows, q, do, mk, kv_all):
     tokens, width = q.shape
     blocks = tokens // BLK
     mem = mk.shape[0]
     heads = width // HD
     nrows = NEAR * BLK
-    qspec = pl.BlockSpec((BLK, HD), lambda h, n, c, t: (n, h))
-    mspec = pl.BlockSpec((mem, HD), lambda h, n, c, t: (0, h))
+    qspec = pl.BlockSpec((BLK, HD), lambda h, n, c, t, f: (n, h))
+    mspec = pl.BlockSpec((mem, HD), lambda h, n, c, t, f: (0, h))
 
     def kv_spec(j, which):
-        return pl.BlockSpec((BLK, HD), lambda h, n, c, t: (t[n * NEAR + j], which * heads + h))
+        return pl.BlockSpec((BLK, HD), lambda h, n, c, t, f: (t[n * NEAR + j], which * heads + h))
 
     anyspec = pl.BlockSpec(memory_space=pl.ANY)
     flops = 2 * tokens * width * (mem + nrows) * 4 + 2 * tokens * width * (nrows * 2 + mem * 2)
     grid_spec = pltpu.PrefetchScalarGridSpec(
-        num_scalar_prefetch=2,
+        num_scalar_prefetch=3,
         grid=(heads, blocks),
         in_specs=[qspec, qspec, mspec]
         + [kv_spec(j, 0) for j in range(NEAR)]
-        + [kv_spec(j, 1) for j in range(NEAR)]
-        + [anyspec],
+        + [kv_spec(j, 1) for j in range(NEAR)],
         out_specs=[qspec, qspec, mspec, anyspec],
         scratch_shapes=[
             pltpu.VMEM((2, NEAR, BLK, HD), jnp.bfloat16),
             pltpu.VMEM((2, NEAR, BLK, HD), jnp.bfloat16),
             pltpu.SemaphoreType.DMA((2, 2 * NEAR)),
+            pltpu.VMEM((BLK, kv_all.shape[1]), jnp.bfloat16),
+            pltpu.SemaphoreType.DMA((free_rows.shape[0],)),
         ],
     )
-    zeros = jnp.zeros(kv_all.shape, jnp.bfloat16)
     return pl.pallas_call(
         _attn_body,
         grid_spec=grid_spec,
@@ -152,7 +171,6 @@
             jax.ShapeDtypeStruct((mem, width), jnp.float32),
             jax.ShapeDtypeStruct(kv_all.shape, jnp.bfloat16),
         ],
-        input_output_aliases={2 + 3 + 2 * NEAR: 3},
         compiler_params=pltpu.CompilerParams(dimension_semantics=("arbitrary", "arbitrary")),
         cost_estimate=pl.CostEstimate(
             flops=flops,
@@ -160,7 +178,7 @@
             bytes_accessed=2 * (4 * tokens * width + mem * width + 4 * blocks * nrows * width)
             + 4 * mem * width,
         ),
-    )(counts, near_rows, q, do, mk, *([kv_all] * (2 * NEAR)), zeros)
+    )(counts, near_rows, free_rows, q, do, mk, *([kv_all] * (2 * NEAR)))
 
 
 def shards(
@@ -202,13 +220,22 @@
     near_block = (near_device * local_blocks + near_slot).astype(jnp.int32)
     my_near = lax.dynamic_slice_in_dim(near_block, my_index * local_blocks, local_blocks, 0).reshape(-1)
     my_count = lax.dynamic_slice_in_dim(near_count, my_index * local_blocks, local_blocks, 0)
+    all_blocks = seq_devices * local_blocks
+    named = jnp.any(my_near[None, :] == jnp.arange(all_blocks)[:, None], axis=1)
+    free_rows = jnp.argsort(named.astype(jnp.int32), stable=True)[: all_blocks - my_near.shape[0]]
+    free_rows = free_rows.astype(jnp.int32)
     attended_rows, query_rows_grad, term, dkv = attention_core(
-        my_count, my_near, queries[0], out_grad[0], memory_keys, kv_all
+        my_count, my_near, free_rows, queries[0], out_grad[0], memory_keys, kv_all
     )
     kv_grad = lax.psum_scatter(dkv, "seq", scatter_dimension=0, tiled=True)
-    row_grads = lax.psum_scatter(
-        term.astype(jnp.bfloat16), "seq", scatter_dimension=0, tiled=True
-    ).astype(jnp.float32)
+    row_parts = lax.all_to_all(
+        term.astype(jnp.bfloat16).reshape(seq_devices, rows_dev, row_width),
+        "seq",
+        split_axis=0,
+        concat_axis=0,
+        tiled=True,
+    )
+    row_grads = jnp.sum(row_parts.astype(jnp.float32), axis=0)
     my_writers = (
         lax.dynamic_slice_in_dim(writer_block, my_index * rows_dev, rows_dev, 0)
         - my_index * local_blocks

time: 437 us -> 346 us (0.79)
  waiting for transfers between devices: 332 us -> 240 us
  local copies, waits for them, and re-layouts: 22.3 us -> 9.95 us
  Pallas kernels: 37.1 us -> 42.9 us
  starting transfers between devices: 12.8 us -> 18.1 us
    reduce_scatter x1 -> x0, waiting for transfers between devices: 73.8 us -> none  [shards(): lax.psum_scatter(term.astype(jnp.bfloat16), 'seq', scatter_dimension=0, t...]
    reduce_scatter x1, waiting for transfers between devices: 158 us -> 113 us  [shards(): kv_grad = lax.psum_scatter(dkv, 'seq', scatter_dimension=0, tiled=True)]
    all_to_all x0 -> x1, waiting for transfers between devices: none -> 26.8 us  [shards(): lax.all_to_all(term.astype(jnp.bfloat16).reshape(seq_devices, rows_dev, r...]
    broadcast_in_dim x1 -> x0, local copies, waits for them, and re-layouts: 11 us -> none  [attention_core(): zeros = jnp.zeros(kv_all.shape, jnp.bfloat16)]
    pallas_call x1, Pallas kernels: 37.1 us -> 42.9 us  [attention_core(): pl.pallas_call(_attn_body, grid_spec=grid_spec, out_shape=[jax.ShapeDtype...]
    all_to_all x0 -> x1, starting transfers between devices: none -> 5.35 us  [shards(): lax.all_to_all(term.astype(jnp.bfloat16).reshape(seq_devices, rows_dev, r...]
  transfers between devices with their start and end apart: 5 -> 5, of which waited for: 5 -> 5; matrix products, arithmetic and copies ran while one was open for 4% -> 7% of each run, Pallas kernels for 0% -> 0%
where the time goes in v4:
time: 346 us; the launch traced here: 344 us
  waiting for transfers between devices  240 us (69%)
  Pallas kernels  42.9 us (12%)
  other arithmetic  18.9 us (5%)
  starting transfers between devices  18.1 us (5%)
  between operations  14.2 us (4%)
  local copies, waits for them, and re-layouts  9.95 us (3%)
    reduce_scatter x1, waiting for transfers between devices, shards(): kv_grad = lax.psum_scatter(dkv, 'seq', scatter_dimension=0, tiled=True)  113 us
    all_gather x1, waiting for transfers between devices, shards(): lax.all_gather(jnp.concatenate([key_states[0], value_states[0]], axis=-1)...  87.9 us
    pallas_call x1, Pallas kernels, attention_core(): pl.pallas_call(_attn_body, grid_spec=grid_spec, out_shape=[jax.ShapeDtype...  42.9 us
    all_to_all x1, waiting for transfers between devices, shards(): lax.all_to_all(term.astype(jnp.bfloat16).reshape(seq_devices, rows_dev, r...  26.8 us
    all_to_all x1, starting transfers between devices, shards(): lax.all_to_all(jnp.broadcast_to(value_sums[None], (seq_devices, local_blo...  8.69 us
    all_to_all x1, waiting for transfers between devices, shards(): lax.all_to_all(jnp.broadcast_to(row_grads[None], (batch_devices, rows_dev...  8.58 us
  transfers between devices with their start and end apart: 5, of which 5 were waited for; matrix products, arithmetic and copies ran while one was open for 7% of the time, Pallas kernels for 0%

profile of v4, /device:TPU:7, one launch (start us, length us, event | category | flops | bytes accessed | tf_op | source)
XLA Modules:
  0.0 344.4 jit_solution(18436724451781901072)
XLA Ops:
  7.2 0.0 copy-start.1
  7.2 0.0 copy-start.2
  7.2 0.0 copy-start
  7.2 0.0 copy-start.4
  7.2 0.0 all-gather.2.cloned.1.call-start
  7.3 2.3 pad_maximum_fusion
  9.5 0.0 all-gather.2.cloned.1.call-update
  9.5 1.1 convert_reduce_fusion.1
  10.7 0.8 broadcast_in_dim.51
  11.5 8.7 %all-to-all-start = ((f32[32,2,1024]{2,1,0:T(2,128)}), f32[32,2,1024]{2,1,0:T(2,128)S(1)}, u32[]{:S(2)}, u32[]{:S(2)}) async-start(f32[32,2,1024]{2,1,0:T(2,128)} %broadcast_in_dim.51), calls=%async_computation | async-start | bytes 524288 | tf_op jit(solution)/shard_map/all_to_all | solution.py:210
  20.2 0.0 reduce-scatter.2.cloned.1.call-start
  20.2 0.0 copy-done.1
  20.2 0.0 copy-done.2
  20.2 0.1 constant_dynamic-slice_fusion
  20.3 0.1 copy.15
  20.4 0.1 reshape.72.nb_ref
  20.5 0.0 copy-done
  20.5 0.0 copy-start.3
  20.5 0.1 fusion.1
  20.6 0.0 copy-done.4
  20.6 0.6 dynamic_slice.9.cnt_ref
  21.2 2.0 sort.17
  23.2 4.4 %all-to-all-done = f32[32,2,1024]{2,1,0:T(2,128)S(1)} async-done(((f32[32,2,1024]{2,1,0:T(2,128)}), f32[32,2,1024]{2,1,0:T(2,128)S(1)}, u32[]{:S(2)}, u32[]{:S(2)}) %all-to-all-start) | async-done | bytes 262176 | tf_op jit(solution)/shard_map/all_to_all | solution.py:210
  27.6 0.2 reshape.73
  27.8 5.4 %gather_fusion = f32[1024,1024]{1,0:T(8,128)} fusion(f32[64,1024]{1,0:T(8,128)S(1)} %reshape.73, s32[1024]{0:T(1024)S(1)} %fusion.2), kind=kCustom, calls=%fused_computation | custom fusion | bytes 8392704 | tf_op jit(solution)/shard_map/jit(_take)/gather | solution.py:217
  33.2 0.0 copy-done.3
  33.2 5.6 %add_convert_fusion.mk_ref = bf16[1024,1024]{1,0:T(8,128)(2,1)} fusion(f32[1024,1024]{1,0:T(8,128)} %param.13, f32[1024,1024]{1,0:T(8,128)} %gather_fusion, pred[1024]{0:T(1024)(128)(4,1)S(1)} %compare_and_fusion), kind=kLoop, calls=%fused_computation.2 | loop fusion | flops 4194304 | bytes 10486784 | tf_op jit(solution)/shard_map/convert_element_type | solution.py:217
  38.8 87.9 %all-gather.2.cloned.1.call-done.rest_0_.rest_1_.rest_2_.rest_3_.rest_4_.rest_5_.rest_6_.rest_7_.rest_8_.rest_9_.rest_10_.rest_11_.rest_12_.rest_13_.rest_14_.rest_15_ = bf16[8192,2048]{1,0:T(8,128)(2,1)} async-done(((bf16[256,2048]{1,0:T(8,128)(2,1)}), bf16[8192,2048]{1,0:T(8,128)(2,1)}) %all-gather.2.cloned.1.call-update) | async-done | bytes 33554448 | tf_op jit(solution)/shard_map/all_gather | solution.py:205
  126.7 42.9 %shard_map.128 = (bf16[256,1024]{1,0:T(8,128)(2,1)}, bf16[256,1024]{1,0:T(8,128)(2,1)}, f32[1024,1024]{1,0:T(8,128)}, bf16[8192,2048]{1,0:T(8,128)(2,1)}) custom-call(s32[2]{0:T(128)} %dynamic_slice.9.cnt_ref, s32[16]{0:T(128)} %copy-done.3, s32[48]{0:T(128)} %bitcast.23, bf16[256,1024]{1,0:T(8,128)(2,1)} %bitcast.19, bf16[256,1024]{1,0:T(8,128)(2,1)} %bitcast.20, ...), custom_call_target="tpu_custom_call" | custom-call | flops 6442450944 | bytes 25165824 | tf_op jit(solution)/shard_map/pallas_call | solution.py:165
  169.7 0.0 reduce-scatter.2.cloned.1.call-update
  169.7 3.9 %convert_element_type.37 = bf16[1024,1024]{1,0:T(8,128)(2,1)} convert(f32[1024,1024]{1,0:T(8,128)} %get-tuple-element.14) | non-fusion elementwise | flops 1048576 | bytes 6291456 | tf_op jit(solution)/shard_map/convert_element_type | solution.py:232
  173.5 5.3 %all-to-all-start.1 = ((bf16[32,32,1024]{2,1,0:T(8,128)(2,1)}), bf16[32,32,1024]{2,1,0:T(8,128)(2,1)S(1)}, u32[]{:S(2)}, u32[]{:S(2)}) async-start(bf16[32,32,1024]{2,1,0:T(8,128)(2,1)} %bitcast.8), calls=%async_computation.2 | async-start | bytes 4194304 | tf_op jit(solution)/shard_map/all_to_all | solution.py:231
  178.9 0.8 dynamic-slice_subtract_fusion
  179.7 26.8 %all-to-all-done.1 = bf16[32,32,1024]{2,1,0:T(8,128)(2,1)S(1)} async-done(((bf16[32,32,1024]{2,1,0:T(8,128)(2,1)}), bf16[32,32,1024]{2,1,0:T(8,128)(2,1)S(1)}, u32[]{:S(2)}, u32[]{:S(2)}) %all-to-all-start.1) | async-done | bytes 2097184 | tf_op jit(solution)/shard_map/all_to_all | solution.py:231
  206.5 0.4 convert_reduce_fusion
  206.9 0.8 broadcast_in_dim.57
  207.7 4.0 %all-to-all-start.2 = ((f32[4,32,1024]{2,1,0:T(8,128)}), f32[4,32,1024]{2,1,0:T(8,128)S(1)}, u32[]{:S(2)}, u32[]{:S(2)}) async-start(f32[4,32,1024]{2,1,0:T(8,128)} %broadcast_in_dim.57), calls=%async_computation.3 | async-start | bytes 1048576 | tf_op jit(solution)/shard_map/all_to_all | solution.py:245
  211.7 0.1 select_reduce_fusion
  211.8 8.6 %all-to-all-done.2 = f32[4,32,1024]{2,1,0:T(8,128)S(1)} async-done(((f32[4,32,1024]{2,1,0:T(8,128)}), f32[4,32,1024]{2,1,0:T(8,128)S(1)}, u32[]{:S(2)}, u32[]{:S(2)}) %all-to-all-start.2) | async-done | bytes 524320 | tf_op jit(solution)/shard_map/all_to_all | solution.py:245
  220.4 0.7 reduce_sum.39
  221.1 112.6 %reduce-scatter.2.cloned.1.call-done = bf16[256,2048]{1,0:T(8,128)(2,1)} async-done(((bf16[8192,2048]{1,0:T(8,128)(2,1)}), bf16[256,2048]{1,0:T(8,128)(2,1)}) %reduce-scatter.2.cloned.1.call-update) | async-done | bytes 1048592 | tf_op jit(solution)/shard_map/reduce_scatter | solution.py:230
  333.7 1.9 slice_bitcast_fusion
  335.6 2.0 fusion
  (7 shorter events, 0.0 us)
Async XLA Ops:
  7.2 13.0 %copy-start.1 = (s32[64,8]{0,1:T(8,128)S(1)}, s32[64,8]{0,1:T(8,128)}, u32[]{:S(2)}) copy-start(s32[64,8]{0,1:T(8,128)} %param.15) | copy-start | bytes 6148
  7.2 13.0 %copy-start.2 = (s32[64,8]{0,1:T(8,128)S(1)}, s32[64,8]{0,1:T(8,128)}, u32[]{:S(2)}) copy-start(s32[64,8]{0,1:T(8,128)} %param.14) | copy-start | bytes 6148
  7.2 13.3 %copy-start = (s32[1024]{0:T(1024)S(1)}, s32[1024]{0:T(1024)}, u32[]{:S(2)}) copy-start(s32[1024]{0:T(1024)} %param.17) | copy-start | bytes 12292
  7.2 13.4 %copy-start.4 = (s32[64]{0:T(128)S(1)}, s32[64]{0:T(128)}, u32[]{:S(2)}) copy-start(s32[64]{0:T(128)} %param.16) | copy-start | bytes 772
  7.2 119.5 %all-gather.2.cloned.1.call-start = ((), (), s32[]{:S(2)}) async-start(), calls=%async_computation.4 | async-start | bytes 34603008 | tf_op jit(solution)/shard_map/all_gather | solution.py:205
  11.5 16.1 %all-to-all-start = ((f32[32,2,1024]{2,1,0:T(2,128)}), f32[32,2,1024]{2,1,0:T(2,128)S(1)}, u32[]{:S(2)}, u32[]{:S(2)}) async-start(f32[32,2,1024]{2,1,0:T(2,128)} %broadcast_in_dim.51), calls=%async_computation | async-start | bytes 524288 | tf_op jit(solution)/shard_map/all_to_all | solution.py:210
  20.2 313.5 %reduce-scatter.2.cloned.1.call-start = ((), (), s32[]{:S(2)}) async-start(), calls=%async_computation.5 | async-start | bytes 34603008 | tf_op jit(solution)/shard_map/reduce_scatter | solution.py:230
  20.5 12.7 %copy-start.3 = (s32[16]{0:T(128)}, s32[16]{0:T(128)S(1)}, u32[]{:S(2)}) copy-start(s32[16]{0:T(128)S(1)} %reshape.72.nb_ref) | copy-start | bytes 196
  173.5 33.0 %all-to-all-start.1 = ((bf16[32,32,1024]{2,1,0:T(8,128)(2,1)}), bf16[32,32,1024]{2,1,0:T(8,128)(2,1)S(1)}, u32[]{:S(2)}, u32[]{:S(2)}) async-start(bf16[32,32,1024]{2,1,0:T(8,128)(2,1)} %bitcast.8), calls=%async_computation.2 | async-start | bytes 4194304 | tf_op jit(solution)/shard_map/all_to_all | solution.py:231
  207.7 12.7 %all-to-all-start.2 = ((f32[4,32,1024]{2,1,0:T(8,128)}), f32[4,32,1024]{2,1,0:T(8,128)S(1)}, u32[]{:S(2)}, u32[]{:S(2)}) async-start(f32[4,32,1024]{2,1,0:T(8,128)} %broadcast_in_dim.57), calls=%async_computation.3 | async-start | bytes 1048576 | tf_op jit(solution)/shard_map/all_to_all | solution.py:245
Sparse Core Ops, SparseCore 0:
  10.3 116.3 all-gather.1
  169.8 163.8 reduce-scatter.1
